TPU v7x, 32 devices: a whole 2x2x4 slice. The times are simulated.
32 devices in a mesh: width: 4 (over z), token: 4 (over y, core), query: 2 (over x).
Axes of the slice: x: 2, y: 2, z: 4, core: 2. Of those that a mesh axis runs over, the one named last changes fastest.
Arguments:
- layer_inputs: bfloat16 [1536, 8192], P(('token', 'query'), 'width'), may hold values from -20 to 20
- out_grads: bfloat16 [1536, 8192], P(('token', 'query'), 'width'), may hold values from -20 to 20
- basis_in: bfloat16 [8192, 8192], P(None, 'width'), may hold values from -0.125 to 0.125
- basis_out: bfloat16 [8192, 8192], P(None, 'width'), may hold values from -0.125 to 0.125
- query_in: bfloat16 [256, 32, 8192], P('query', None, 'width'), may hold values from -0.03125 to 0.03125
- query_out: bfloat16 [256, 32, 8192], P('query', None, 'width'), may hold values from -0.03125 to 0.03125
Outputs:
- scores: float32 [256, 1536], P('query', 'token')
All inputs are finite; a program needn't handle non-finite values.
Results may differ from a plain program's by a relative error of at most 0.0003.
Values may be sent and summed in bfloat16 or wider, within the bound.
No kernel may reach another device: no remote copies, remote signals or barrier semaphores. Data moves between devices by JAX's collectives and lax.ppermute only.
A program may use at most 192 MiB of HBM per device.

v0:
```python
import jax
import jax.numpy as jnp
from jax import lax
from jax.experimental import pallas as pl
from jax.experimental.pallas import tpu as pltpu
from jax.sharding import PartitionSpec as P


damping = 0.1
reach = 172.0
floor = 1e-30
scale_rows = 16
basis_block = 1024
basis_streams = 2
split_block = 512
chunks = 4
groups_in = ((0, 1), (2, 3))
groups_out = ((0, 1), (2,), (3,))


def swap_pairs(count):
    even = [(i, i ^ 1) for i in range(count)]
    odd = [(0, 0), (count - 1, count - 1)] + [(i, i + 1 if i % 2 else i - 1) for i in range(1, count - 1)]
    return even, odd


def shift_pairs(count, by):
    return [(i, (i + by) % count) for i in range(count)]


def line_sources(width, place):
    got = []
    for distance in range(1, width):
        right, left = place + distance, place - distance
        pair = (right, left) if place % 2 == 0 else (left, right)
        got += [pair[0]] if distance == width - 1 else list(pair)
    return [source if 0 <= source < width else None for source in got]


def rotate_plan(width, nk):
    rows = []
    for place in range(width):
        sources = [place] + line_sources(width, place)
        blocks, hold = [], 0
        for source in sources:
            for k in range(nk):
                hold = hold if source is None else source * nk + k
                blocks.append(hold)
        rows.append(blocks + [int(source is not None) for source in sources])
    return rows


def rotate_step(acc, first, buffers, basis, plan, count, last):
    tokens, depth = buffers[0].shape
    cols = basis.shape[1]
    bk = min(basis_block, depth)
    nk = depth // bk
    n = len(buffers)
    has_acc = acc is not None

    def body(plan_ref, *refs):
        chunk_refs, refs = refs[:n], refs[n:]
        if n > 1:
            picked_ref, refs = refs[-1], refs[:-1]
        basis_refs = refs[:basis_streams]
        acc_ref = refs[basis_streams] if has_acc else None
        out_refs = refs[basis_streams + has_acc :]
        out_ref = out_refs[0]
        c, k = pl.program_id(0), pl.program_id(1)

        @pl.when((c == 0) & (k == 0))
        def _():
            if has_acc:
                out_ref[...] = acc_ref[...]
            else:
                out_ref[...] = jnp.zeros_like(out_ref)

        if n > 1:
            for i in range(n):
                @pl.when(c == i)
                def _():
                    picked_ref[...] = chunk_refs[i][...]

        @pl.when(plan_ref[count * nk + first + c] > 0)
        def _():
            chunk_ref = picked_ref if n > 1 else chunk_refs[0]
            piece = bk // basis_streams
            total = out_ref[...]
            for j in range(basis_streams):
                total += jnp.dot(
                    chunk_ref[:, j * piece : (j + 1) * piece], basis_refs[j][...], preferred_element_type=jnp.float32
                )
            out_ref[...] = total

        if last:
            @pl.when((c == n - 1) & (k == nk - 1))
            def _():
                total = out_ref[...]
                out_refs[1][...] = jnp.sum(total * total, axis=0, keepdims=True)
                encode(total, out_refs[2])

    whole = pl.BlockSpec((tokens, cols), lambda c, k, s: (0, 0))
    in_specs = []
    for i in range(n):
        in_specs.append(
            pl.BlockSpec(
                (tokens, bk), lambda c, k, s, i=i: (0, jnp.where(c == i, k, jnp.where(c < i, 0, nk - 1)))
            )
        )
    for j in range(basis_streams):
        in_specs.append(
            pl.BlockSpec(
                (bk // basis_streams, cols),
                lambda c, k, s, j=j: (s[(first + c) * nk + k] * basis_streams + j, 0),
            )
        )
    operands = [*buffers, *[basis] * basis_streams]
    if has_acc:
        in_specs.append(whole)
        operands.append(acc)
    out_shape = [jax.ShapeDtypeStruct((tokens, cols), jnp.float32)]
    out_specs = [whole]
    if last:
        out_shape.append(jax.ShapeDtypeStruct((1, cols), jnp.float32))
        out_specs.append(pl.BlockSpec((1, cols), lambda c, k, s: (0, 0)))
        out_shape.append(jax.ShapeDtypeStruct((tokens + scale_rows, cols), jnp.bfloat16))
        out_specs.append(pl.BlockSpec((tokens + scale_rows, cols), lambda c, k, s: (0, 0)))
    out = pl.pallas_call(
        body,
        out_shape=out_shape,
        grid_spec=pltpu.PrefetchScalarGridSpec(
            num_scalar_prefetch=1,
            grid=(n, nk),
            in_specs=in_specs,
            out_specs=out_specs,
            scratch_shapes=[pltpu.VMEM((tokens, bk), jnp.bfloat16)] if n > 1 else [],
        ),
        compiler_params=pltpu.CompilerParams(dimension_semantics=("arbitrary", "arbitrary")),
        cost_estimate=pl.CostEstimate(
            flops=4 * tokens * depth * cols, transcendentals=0, bytes_accessed=2 * depth * cols * 2 + tokens * cols * 8
        ),
        name="rotate",
    )(plan, *operands)
    return out if last else out[0]


def encode(value, out_ref):
    count = value.shape[0]
    top = jnp.max(jnp.abs(value), axis=0, keepdims=True)
    top = jnp.maximum(top * (1 + 2.0**-7), floor).astype(jnp.bfloat16)
    size = jnp.exp(jnp.abs(value) * (reach / top.astype(jnp.float32)) - reach / 2)
    out_ref[:count, :] = jnp.where(value < 0, -size, size).astype(jnp.bfloat16)
    out_ref[count:, :] = jnp.broadcast_to(top, (scale_rows, value.shape[1]))


def decode(ref):
    count = ref.shape[0] - scale_rows
    code = ref[:count, :].astype(jnp.float32)
    top = ref[count : count + 1, :].astype(jnp.float32)
    size = (jnp.log(jnp.abs(code)) + reach / 2) * (top * (1.0 / reach))
    return jnp.where(code < 0, -size, size)


def split_scaled(rotated, codes, squares, place, total_tokens):
    n = 1 + len(codes)
    tokens, cols = rotated.shape
    bc = min(split_block, cols)

    def body(place_ref, *refs):
        out_ref = refs[-1]
        squares_total = refs[0][...]
        for ref in refs[1 : len(squares)]:
            squares_total += ref[...]
        refs = refs[len(squares) :]
        gain = 1.0 / (squares_total / total_tokens + damping)
        for by in range(n):
            scaled = (refs[0][...] if by == 0 else decode(refs[by])) * gain
            head = scaled.astype(jnp.bfloat16)
            slot = lax.rem(place_ref[0] + (n - by), n) * tokens
            rows = pl.ds(pl.multiple_of(slot, tokens), tokens)
            out_ref[0, rows, :] = head
            out_ref[1, rows, :] = (scaled - head.astype(jnp.float32)).astype(jnp.bfloat16)

    in_specs = [pl.BlockSpec((1, bc), lambda b, s: (0, b)) for _ in squares]
    in_specs.append(pl.BlockSpec((tokens, bc), lambda b, s: (0, b)))
    for _ in codes:
        in_specs.append(pl.BlockSpec((tokens + scale_rows, bc), lambda b, s: (0, b)))
    return pl.pallas_call(
        body,
        out_shape=jax.ShapeDtypeStruct((2, n * tokens, cols), jnp.bfloat16),
        grid_spec=pltpu.PrefetchScalarGridSpec(
            num_scalar_prefetch=1,
            grid=(cols // bc,),
            in_specs=in_specs,
            out_specs=pl.BlockSpec((2, n * tokens, bc), lambda b, s: (0, 0, b)),
        ),
        compiler_params=pltpu.CompilerParams(dimension_semantics=("arbitrary",)),
        cost_estimate=pl.CostEstimate(
            flops=8 * n * tokens * cols, transcendentals=n * tokens * cols, bytes_accessed=8 * n * tokens * cols
        ),
        name="split",
    )(place, *squares, rotated, *codes)


def mirror(place, width):
    part, step = 0, 1
    while step < width:
        part = 2 * part + place // step % 2
        step *= 2
    return part


def pair_plan(width, size):
    rows = []
    for place in range(width):
        lo, count, kept, steps, step = 0, width, [], [], 1
        while step <= width:
            count //= 2
            upper = place // step % 2
            start_at = lo + (1 - upper) * count
            if step == width:
                start_at, count = lo, 1
            steps.append(
                [
                    [c * width + start_at + i] + [c * many + start_at + i - base for base, many in kept]
                    for c in range(size)
                    for i in range(count)
                ]
            )
            lo += upper * count if step < width else 0
            kept.append((lo, count))
            step *= 2
        rows.append(steps)
    return rows


def pair_step(rows, scaled, received, plan, first, shift, nb, block, mode, other=None, rank_count=None):
    depth = rows.shape[1]
    group = scaled.shape[1]
    n = len(received)
    length = nb * block

    def body(plan_ref, row_ref, scaled_ref, *refs):
        both = scaled_ref[...].reshape(2 * group, depth)
        product = lax.dot_general(
            row_ref[...], both, (((1,), (1,)), ((), ())), preferred_element_type=jnp.float32
        )
        total = product[:, :group] + product[:, group:]
        for i in range(n):
            total = total + decode(refs[i])
        out_ref = refs[-1]
        if mode == "code":
            encode(total, out_ref)
        elif mode == "plain":
            out_ref[...] = total
        else:
            joined = total * refs[n][...]
            out_ref[0] = jnp.sum(joined.reshape(block // rank_count, rank_count, group), axis=1)

    def place_of(column):
        return lambda b, s: (s[first + b * (n + 1) + column] + (shift if column == 0 else 0), 0)

    in_specs = [
        pl.BlockSpec((block, depth), place_of(0)),
        pl.BlockSpec((2, group, depth), lambda b, s: (0, 0, 0), pipeline_mode=pl.Buffered(1)),
    ]
    for i in range(n):
        in_specs.append(pl.BlockSpec((block + scale_rows, group), place_of(1 + i)))
    operands = [rows, scaled, *received]
    if mode == "code":
        out_shape = jax.ShapeDtypeStruct((nb * (block + scale_rows), group), jnp.bfloat16)
        out_spec = pl.BlockSpec((block + scale_rows, group), lambda b, s: (b, 0))
    elif mode == "plain":
        out_shape = jax.ShapeDtypeStruct((length, group), jnp.float32)
        out_spec = pl.BlockSpec((block, group), lambda b, s: (b, 0))
    else:
        other, at = other
        in_specs.append(pl.BlockSpec((block, group), lambda b, s: (at + b, 0)))
        operands.append(other)
        out_shape = jax.ShapeDtypeStruct((nb, block // rank_count, group), jnp.float32)
        out_spec = pl.BlockSpec((1, block // rank_count, group), lambda b, s: (b, 0, 0))
    return pl.pallas_call(
        body,
        out_shape=out_shape,
        grid_spec=pltpu.PrefetchScalarGridSpec(
            num_scalar_prefetch=1, grid=(nb,), in_specs=in_specs, out_specs=out_spec
        ),
        compiler_params=pltpu.CompilerParams(dimension_semantics=("arbitrary",)),
        cost_estimate=pl.CostEstimate(
            flops=4 * length * depth * group,
            transcendentals=2 * length * group,
            bytes_accessed=length * depth * 2 + 2 * group * depth * 2,
        ),
    )(plan, *operands)


def reduce_pairs(members, rows, scaled, plan, firsts, block, width, other=None, rank_count=None):
    received = []
    step, nb, shift = 1, len(members) * width, members[0] * width
    while step < width:
        nb //= 2
        code = pair_step(rows, scaled, received, plan, firsts[len(received)], shift, nb, block, "code")
        pairs = [(i, i ^ step) for i in range(width)]
        received = received + [in_hbm(lax.ppermute(code, "width", pairs))]
        step *= 2
    mode = "plain" if other is None else "joined"
    return pair_step(
        rows, scaled, received, plan, firsts[len(received)], shift, nb, block, mode, other, rank_count
    )


def assemble(batches, plan, first):
    width = len(batches[0])
    arrays = [array for batch in batches for array in batch]
    total = sum(batch[0].shape[0] for batch in batches)

    def body(plan_ref, *refs):
        out_ref = refs[-1]
        base = 0
        for b, batch in enumerate(batches):
            size = batch[0].shape[0]
            for x in range(width):
                for c in range(size):
                    out_ref[base + c, pl.ds(plan_ref[first + x], 1)] = refs[b * width + x][pl.ds(c, 1)]
            base += size

    return pl.pallas_call(
        body,
        out_shape=jax.ShapeDtypeStruct((total, width) + arrays[0].shape[1:], jnp.float32),
        in_specs=[pl.BlockSpec(memory_space=pltpu.SMEM)] + [pl.BlockSpec(memory_space=pltpu.VMEM)] * len(arrays),
        out_specs=pl.BlockSpec(memory_space=pltpu.VMEM),
        name="assemble",
    )(plan, *arrays)


def in_hbm(x):
    return pltpu.with_memory_space_constraint(x, pltpu.HBM)


def gather_rotate(own, basis, plan, width):
    even, odd = swap_pairs(width)
    count = 2 * width - 2
    send_even = send_odd = own
    acc = rotate_step(None, 0, [own], basis, plan, count, width == 1)
    for distance in range(1, width):
        last = distance == width - 1
        got = [lax.ppermute(send_even, "width", even)]
        if not last:
            got.append(lax.ppermute(send_odd, "width", odd))
            send_even, send_odd = got[1], got[0]
        acc = rotate_step(acc, 2 * distance - 1, [in_hbm(x) for x in got], basis, plan, count, last)
    return acc


def scaled_group(rotated, squares, code, place, total_tokens):
    query_count, token_count = lax.axis_size("query"), lax.axis_size("token")
    codes, total = [], squares
    for by in range(1, query_count):
        shifted = shift_pairs(query_count, by)
        codes.append(in_hbm(lax.ppermute(code, "query", shifted)))
        total = total + lax.ppermute(squares, "query", shifted)
    sums = [total] + [lax.ppermute(total, "token", shift_pairs(token_count, by)) for by in range(1, token_count)]
    return split_scaled(rotated, codes, sums, place, total_tokens)


def compute(layer_inputs, out_grads, basis_in, basis_out, query_in, query_out):
    width = lax.axis_size("width")
    place = lax.axis_index("width")
    total_tokens = layer_inputs.shape[0] * lax.axis_size("token") * lax.axis_size("query")
    queries, rank_count, width_cols = query_in.shape
    rows_in = query_in.reshape(-1, width_cols)
    rows_out = query_out.reshape(-1, width_cols)
    block = rows_in.shape[0] // (chunks * width)

    depth = layer_inputs.shape[1]
    table = rotate_plan(width, depth // min(basis_block, depth))
    firsts = {}
    for size in sorted({len(members) for members in groups_in + groups_out}):
        firsts[size] = []
        for step in range(len(pair_plan(width, size)[0])):
            firsts[size].append(len(table[0]))
            for at, steps in enumerate(pair_plan(width, size)):
                table[at] += [number for entry in steps[step] for number in entry]
    parts_at = len(table[0])
    for at in range(width):
        table[at] += [mirror(at ^ x, width) for x in range(width)]
    plan = lax.dynamic_index_in_dim(jnp.asarray(table, jnp.int32), place, keepdims=False)
    query_place = lax.axis_index("query").astype(jnp.int32)[None]

    got_in = gather_rotate(layer_inputs, basis_in, plan, width)
    got_out = gather_rotate(out_grads, basis_out, plan, width)
    scaled_in = scaled_group(*got_in, query_place, total_tokens)
    scaled_out = scaled_group(*got_out, query_place, total_tokens)

    found = {}
    for members in groups_in:
        pairs = reduce_pairs(members, rows_in, scaled_in, plan, firsts[len(members)], block, width)
        found.update({c: (pairs, i) for i, c in enumerate(members)})
    batches = []
    for members in groups_out:
        own = reduce_pairs(
            members, rows_out, scaled_out, plan, firsts[len(members)], block, width, found[members[0]], rank_count
        )
        batches.append(
            [own] + [lax.ppermute(own, "width", [(i, i ^ x) for i in range(width)]) for x in range(1, width)]
        )
    scores = assemble(batches, plan, parts_at)
    return scores.reshape(queries, scores.shape[-1])


def solution(mesh):
    return jax.shard_map(
        compute,
        mesh=mesh,
        in_specs=(
            P(("token", "query"), "width"),
            P(("token", "query"), "width"),
            P(None, "width"),
            P(None, "width"),
            P("query", None, "width"),
            P("query", None, "width"),
        ),
        out_specs=P("query", "token"),
        check_vma=False,
    )
```

profile of v0, /device:TPU:0, one launch (start us, length us, event | category | flops | bytes accessed | tf_op | source)
XLA Modules:
  0.0 317.3 jit_solution(5013612485343330058)
XLA Ops:
  0.0 3.1 collective-permute-start.12
  3.1 1.8 collective-permute-start.15
  4.8 3.3 %collective-permute-start = (bf16[192,2048]{1,0:T(8,128)(2,1)}, bf16[192,2048]{1,0:T(8,128)(2,1)S(1)}, u32[]{:S(2)}, u32[]{:S(2)}) collective-permute-start(bf16[192,2048]{1,0:T(8,128)(2,1)} %refs_0_.2), channel_id=1, source_target_pairs={{0,8},{8,0},{16,24},{24,16},{1,9},{9,1},{17,25},{25,17},{2,10},{10... | collective-permute-start | bytes 2359304 | tf_op jit(solution)/shard_map/ppermute | solution.py:347
  8.2 13.6 %collective-permute-done.12.refs_0_ = bf16[192,2048]{1,0:T(8,128)(2,1)} collective-permute-done((bf16[192,2048]{1,0:T(8,128)(2,1)}, bf16[192,2048]{1,0:T(8,128)(2,1)}, u32[]{:S(2)}, u32[]{:S(2)}) %collective-permute-start.12) | collective-permute-done | bytes 786464 | tf_op jit(solution)/shard_map/ppermute | solution.py:347
  21.8 1.8 collective-permute-start.13
  23.5 1.8 collective-permute-start.3
  26.5 4.3 %collective-permute-start.16 = (bf16[192,2048]{1,0:T(8,128)(2,1)S(1)}, bf16[192,2048]{1,0:T(8,128)(2,1)}, u32[]{:S(2)}, u32[]{:S(2)}) collective-permute-start(bf16[192,2048]{1,0:T(8,128)(2,1)S(1)} %collective-permute-done.15.refs_1_), channel_id=1, source_target_pairs={{0,8},{8,0},{16,24},{24,16},{1,9},{9,1},{17,25},{25,17},{2,10},{10... | collective-permute-start | bytes 2359304 | tf_op jit(solution)/shard_map/ppermute | solution.py:347
  30.8 7.7 %collective-permute-done.refs_0_ = bf16[192,2048]{1,0:T(8,128)(2,1)S(1)} collective-permute-done((bf16[192,2048]{1,0:T(8,128)(2,1)}, bf16[192,2048]{1,0:T(8,128)(2,1)S(1)}, u32[]{:S(2)}, u32[]{:S(2)}) %collective-permute-start) | collective-permute-done | bytes 786464 | tf_op jit(solution)/shard_map/ppermute | solution.py:347
  40.1 6.5 %rotate.12.refs_4_ = f32[192,2048]{1,0:T(8,128)} custom-call(s32[43]{0:T(128)} %dynamic-slice_bitcast_fusion.plan_ref, bf16[192,2048]{1,0:T(8,128)(2,1)} %refs_0_.3, bf16[8192,2048]{1,0:T(8,128)(2,1)} %refs_2_.15, bf16[8192,2048]{1,0:T(8,128)(2,1)} %refs_2_.15), custom_call_target="tpu_custom_call" | custom-call | flops 3221225472 | bytes 19922944 | tf_op jit(solution)/shard_map/rotate/pallas_call | solution.py:128
  46.6 4.0 %collective-permute-start.14 = (bf16[192,2048]{1,0:T(8,128)(2,1)S(1)}, bf16[192,2048]{1,0:T(8,128)(2,1)}, u32[]{:S(2)}, u32[]{:S(2)}) collective-permute-start(bf16[192,2048]{1,0:T(8,128)(2,1)S(1)} %collective-permute-done.13.refs_1_), channel_id=1, source_target_pairs={{0,8},{8,0},{16,24},{24,16},{1,9},{9,1},{17,25},{25,17},{2,10},{10... | collective-permute-start | bytes 2359304 | tf_op jit(solution)/shard_map/ppermute | solution.py:347
  50.6 6.6 %rotate.8.refs_4_ = f32[192,2048]{1,0:T(8,128)} custom-call(s32[43]{0:T(128)} %dynamic-slice_bitcast_fusion.plan_ref, bf16[192,2048]{1,0:T(8,128)(2,1)} %refs_0_.2, bf16[8192,2048]{1,0:T(8,128)(2,1)} %refs_2_.11, bf16[8192,2048]{1,0:T(8,128)(2,1)} %refs_2_.11), custom_call_target="tpu_custom_call" | custom-call | flops 3221225472 | bytes 19922944 | tf_op jit(solution)/shard_map/rotate/pallas_call | solution.py:128
  57.2 5.9 %collective-permute-start.4 = (bf16[192,2048]{1,0:T(8,128)(2,1)S(1)}, bf16[192,2048]{1,0:T(8,128)(2,1)}, u32[]{:S(2)}, u32[]{:S(2)}) collective-permute-start(bf16[192,2048]{1,0:T(8,128)(2,1)S(1)} %collective-permute-done.3.refs_1_), channel_id=1, source_target_pairs={{0,8},{8,0},{16,24},{24,16},{1,9},{9,1},{17,25},{25,17},{2,10},{10... | collective-permute-start | bytes 2359304 | tf_op jit(solution)/shard_map/ppermute | solution.py:347
  63.1 8.2 %rotate.13.refs_4_ = f32[192,2048]{1,0:T(8,128)} custom-call(s32[43]{0:T(128)} %dynamic-slice_bitcast_fusion.plan_ref, bf16[192,2048]{1,0:T(8,128)(2,1)} %collective-permute-done.12.refs_0_, bf16[192,2048]{1,0:T(8,128)(2,1)} %copy-done.9, bf16[8192,2048]{1,0:T(8,128)(2,1)} %refs_2_.15, bf16[8192,2048]{1,0:T(8,128)(2,1)} %refs_2_.15, f32[192,2048]{1,0:T(8,128)} %rotate.12.refs_4_), custom_call_target="tpu_custom_call" | custom-call | flops 3221225472 | bytes 19922944 | tf_op jit(solution)/shard_map/rotate/pallas_call | solution.py:128
  71.4 5.6 %collective-permute-start.2 = (bf16[192,2048]{1,0:T(8,128)(2,1)}, bf16[192,2048]{1,0:T(8,128)(2,1)S(1)}, u32[]{:S(2)}, u32[]{:S(2)}) collective-permute-start(bf16[192,2048]{1,0:T(8,128)(2,1)} %collective-permute-done.1.refs_1_), channel_id=1, source_target_pairs={{0,8},{8,0},{16,24},{24,16},{1,9},{9,1},{17,25},{25,17},{2,10},{10... | collective-permute-start | bytes 2359304 | tf_op jit(solution)/shard_map/ppermute | solution.py:347
  77.0 8.2 %rotate.14.refs_3_ = f32[192,2048]{1,0:T(8,128)} custom-call(s32[43]{0:T(128)} %dynamic-slice_bitcast_fusion.plan_ref, bf16[192,2048]{1,0:T(8,128)(2,1)} %collective-permute-done.16.refs_0_, bf16[192,2048]{1,0:T(8,128)(2,1)} %copy-done.10, bf16[8192,2048]{1,0:T(8,128)(2,1)} %refs_2_.15, bf16[8192,2048]{1,0:T(8,128)(2,1)} %refs_2_.15, f32[192,2048]{1,0:T(8,128)} %rotate.13.refs_4_), custom_call_target="tpu_custom_call" | custom-call | flops 3221225472 | bytes 19922944 | tf_op jit(solution)/shard_map/rotate/pallas_call | solution.py:128
  85.2 8.5 %rotate.15 = (f32[192,2048]{1,0:T(8,128)}, f32[1,2048]{1,0:T(1,128)}, bf16[208,2048]{1,0:T(8,128)(2,1)}) custom-call(s32[43]{0:T(128)} %dynamic-slice_bitcast_fusion.plan_ref, bf16[192,2048]{1,0:T(8,128)(2,1)} %collective-permute-done.14.refs_0_, bf16[8192,2048]{1,0:T(8,128)(2,1)} %refs_2_.15, bf16[8192,2048]{1,0:T(8,128)(2,1)} %refs_2_.15, ...), custom_call_target="tpu_custom_call" | custom-call | flops 3221225472 | bytes 19922944 | tf_op jit(solution)/shard_map/rotate/pallas_call | solution.py:128
  95.2 8.2 %rotate.9.refs_4_ = f32[192,2048]{1,0:T(8,128)} custom-call(s32[43]{0:T(128)} %dynamic-slice_bitcast_fusion.plan_ref, bf16[192,2048]{1,0:T(8,128)(2,1)} %copy-done.7, bf16[192,2048]{1,0:T(8,128)(2,1)} %copy-done.8, bf16[8192,2048]{1,0:T(8,128)(2,1)} %refs_2_.11, bf16[8192,2048]{1,0:T(8,128)(2,1)} %refs_2_.11, f32[192,2048]{1,0:T(8,128)} %rotate.8.refs_4_), custom_call_target="tpu_custom_call" | custom-call | flops 3221225472 | bytes 19922944 | tf_op jit(solution)/shard_map/rotate/pallas_call | solution.py:128
  103.4 8.2 %rotate.10.refs_3_ = f32[192,2048]{1,0:T(8,128)} custom-call(s32[43]{0:T(128)} %dynamic-slice_bitcast_fusion.plan_ref, bf16[192,2048]{1,0:T(8,128)(2,1)} %collective-permute-done.4.refs_0_, bf16[192,2048]{1,0:T(8,128)(2,1)} %collective-permute-done.1.refs_1_, bf16[8192,2048]{1,0:T(8,128)(2,1)} %refs_2_.11, bf16[8192,2048]{1,0:T(8,128)(2,1)} %refs_2_.11, ...), custom_call_target="tpu_custom_call" | custom-call | flops 3221225472 | bytes 19922944 | tf_op jit(solution)/shard_map/rotate/pallas_call | solution.py:128
  112.6 8.5 %rotate.11 = (f32[192,2048]{1,0:T(8,128)}, f32[1,2048]{1,0:T(1,128)}, bf16[208,2048]{1,0:T(8,128)(2,1)}) custom-call(s32[43]{0:T(128)} %dynamic-slice_bitcast_fusion.plan_ref, bf16[192,2048]{1,0:T(8,128)(2,1)} %copy-done.11, bf16[8192,2048]{1,0:T(8,128)(2,1)} %refs_2_.11, bf16[8192,2048]{1,0:T(8,128)(2,1)} %refs_2_.11, f32[192,2048]{1,0:T(8,128)} %rotate.10.refs_3_), custom_call_target="tpu_custom_call" | custom-call | flops 3221225472 | bytes 19922944 | tf_op jit(solution)/shard_map/rotate/pallas_call | solution.py:128
  123.7 15.2 %collective-permute-done.17 = f32[1,2048]{1,0:T(1,128)S(1)} collective-permute-done((f32[1,2048]{1,0:T(1,128)S(1)}, f32[1,2048]{1,0:T(1,128)S(1)}, u32[]{:S(2)}, u32[]{:S(2)}) %collective-permute-start.17) | collective-permute-done | bytes 8224 | tf_op jit(solution)/shard_map/ppermute | solution.py:361
  146.0 4.6 %split.3.scaled_ref = bf16[2,384,2048]{2,1,0:T(8,128)(2,1)} custom-call(s32[1]{0:T(128)} %bitcast.2.place_ref, f32[1,2048]{1,0:T(1,128)} %copy-done.19, f32[1,2048]{1,0:T(1,128)} %copy-done.30, f32[1,2048]{1,0:T(1,128)} %copy-done.32, f32[1,2048]{1,0:T(1,128)} %copy-done.34, f32[192,2048]{1,0:T(8,128)} %get-tuple-element.15.refs_4_, bf16[208,2048]{1,0:T(8,128)(2,1)} %copy-done.6), custom_call_target="tpu_custom_call" | custom-call | flops 6291456 | bytes 6291456 | tf_op jit(solution)/shard_map/split/pallas_call | solution.py:188
  150.6 8.4 %shard_map.81 = bf16[1088,384]{1,0:T(8,128)(2,1)} custom-call(s32[43]{0:T(128)} %dynamic-slice_bitcast_fusion.plan_ref, bf16[4096,2048]{1,0:T(8,128)(2,1)} %bitcast.15, bf16[2,384,2048]{2,1,0:T(8,128)(2,1)} %split.3.scaled_ref), custom_call_target="tpu_custom_call" | custom-call | flops 3221225472 | bytes 7340032 | tf_op jit(solution)/shard_map/pallas_call | solution.py:282
  159.4 8.4 %shard_map.75 = bf16[1088,384]{1,0:T(8,128)(2,1)} custom-call(s32[43]{0:T(128)} %dynamic-slice_bitcast_fusion.plan_ref, bf16[4096,2048]{1,0:T(8,128)(2,1)} %bitcast.16, bf16[2,384,2048]{2,1,0:T(8,128)(2,1)} %split.3.scaled_ref), custom_call_target="tpu_custom_call" | custom-call | flops 3221225472 | bytes 7340032 | tf_op jit(solution)/shard_map/pallas_call | solution.py:282
  167.9 1.6 collective-permute-start.22
  170.4 4.6 %split.2.scaled_ref = bf16[2,384,2048]{2,1,0:T(8,128)(2,1)} custom-call(s32[1]{0:T(128)} %bitcast.2.place_ref, f32[1,2048]{1,0:T(1,128)} %copy-done.18, f32[1,2048]{1,0:T(1,128)} %copy-done.29, f32[1,2048]{1,0:T(1,128)} %copy-done.31, f32[1,2048]{1,0:T(1,128)} %copy-done.33, f32[192,2048]{1,0:T(8,128)} %get-tuple-element.12.refs_4_, bf16[208,2048]{1,0:T(8,128)(2,1)} %copy-done.5), custom_call_target="tpu_custom_call" | custom-call | flops 6291456 | bytes 6291456 | tf_op jit(solution)/shard_map/split/pallas_call | solution.py:188
  175.1 8.5 %shard_map.73 = bf16[1088,384]{1,0:T(8,128)(2,1)} custom-call(s32[43]{0:T(128)} %dynamic-slice_bitcast_fusion.plan_ref, bf16[4096,2048]{1,0:T(8,128)(2,1)} %bitcast.6, bf16[2,384,2048]{2,1,0:T(8,128)(2,1)} %split.2.scaled_ref), custom_call_target="tpu_custom_call" | custom-call | flops 3221225472 | bytes 7340032 | tf_op jit(solution)/shard_map/pallas_call | solution.py:282
  184.0 5.9 %shard_map.85 = bf16[544,384]{1,0:T(8,128)(2,1)} custom-call(s32[43]{0:T(128)} %dynamic-slice_bitcast_fusion.plan_ref, bf16[4096,2048]{1,0:T(8,128)(2,1)} %bitcast.7, bf16[2,384,2048]{2,1,0:T(8,128)(2,1)} %split.2.scaled_ref), custom_call_target="tpu_custom_call" | custom-call | flops 1610612736 | bytes 5242880 | tf_op jit(solution)/shard_map/pallas_call | solution.py:282
  189.9 1.6 collective-permute-start.34
  191.5 5.9 %shard_map.79 = bf16[544,384]{1,0:T(8,128)(2,1)} custom-call(s32[43]{0:T(128)} %dynamic-slice_bitcast_fusion.plan_ref, bf16[4096,2048]{1,0:T(8,128)(2,1)} %bitcast.8, bf16[2,384,2048]{2,1,0:T(8,128)(2,1)} %split.2.scaled_ref), custom_call_target="tpu_custom_call" | custom-call | flops 1610612736 | bytes 5242880 | tf_op jit(solution)/shard_map/pallas_call | solution.py:282
  198.8 6.2 %shard_map.82 = bf16[544,384]{1,0:T(8,128)(2,1)} custom-call(s32[43]{0:T(128)} %dynamic-slice_bitcast_fusion.plan_ref, bf16[4096,2048]{1,0:T(8,128)(2,1)} %bitcast.17, bf16[2,384,2048]{2,1,0:T(8,128)(2,1)} %split.3.scaled_ref, bf16[1088,384]{1,0:T(8,128)(2,1)} %copy-done.2), custom_call_target="tpu_custom_call" | custom-call | flops 1610612736 | bytes 5242880 | tf_op jit(solution)/shard_map/pallas_call | solution.py:282
  204.9 2.6 collective-permute-start.30
  207.5 26.9 %collective-permute-done.34.refs_0_ = bf16[544,384]{1,0:T(8,128)(2,1)S(1)} collective-permute-done((bf16[544,384]{1,0:T(8,128)(2,1)}, bf16[544,384]{1,0:T(8,128)(2,1)S(1)}, u32[]{:S(2)}, u32[]{:S(2)}) %collective-permute-start.34) | collective-permute-done | bytes 417824 | tf_op jit(solution)/shard_map/ppermute | solution.py:304
  235.2 4.8 %shard_map.86 = bf16[272,384]{1,0:T(8,128)(2,1)} custom-call(s32[43]{0:T(128)} %dynamic-slice_bitcast_fusion.plan_ref, bf16[4096,2048]{1,0:T(8,128)(2,1)} %bitcast.9, bf16[2,384,2048]{2,1,0:T(8,128)(2,1)} %split.2.scaled_ref, bf16[544,384]{1,0:T(8,128)(2,1)} %copy-done.4), custom_call_target="tpu_custom_call" | custom-call | flops 805306368 | bytes 4194304 | tf_op jit(solution)/shard_map/pallas_call | solution.py:282
  242.9 4.8 %shard_map.80 = bf16[272,384]{1,0:T(8,128)(2,1)} custom-call(s32[43]{0:T(128)} %dynamic-slice_bitcast_fusion.plan_ref, bf16[4096,2048]{1,0:T(8,128)(2,1)} %bitcast.10, bf16[2,384,2048]{2,1,0:T(8,128)(2,1)} %split.2.scaled_ref, bf16[544,384]{1,0:T(8,128)(2,1)} %copy-done.3), custom_call_target="tpu_custom_call" | custom-call | flops 805306368 | bytes 4194304 | tf_op jit(solution)/shard_map/pallas_call | solution.py:282
  249.3 6.1 %shard_map.76 = bf16[544,384]{1,0:T(8,128)(2,1)} custom-call(s32[43]{0:T(128)} %dynamic-slice_bitcast_fusion.plan_ref, bf16[4096,2048]{1,0:T(8,128)(2,1)} %bitcast.18, bf16[2,384,2048]{2,1,0:T(8,128)(2,1)} %split.3.scaled_ref, bf16[1088,384]{1,0:T(8,128)(2,1)} %copy-done.1), custom_call_target="tpu_custom_call" | custom-call | flops 1610612736 | bytes 5242880 | tf_op jit(solution)/shard_map/pallas_call | solution.py:282
  255.5 2.2 collective-permute-start.23
  258.6 6.1 %shard_map.74 = bf16[544,384]{1,0:T(8,128)(2,1)} custom-call(s32[43]{0:T(128)} %dynamic-slice_bitcast_fusion.plan_ref, bf16[4096,2048]{1,0:T(8,128)(2,1)} %bitcast.11, bf16[2,384,2048]{2,1,0:T(8,128)(2,1)} %split.2.scaled_ref, bf16[1088,384]{1,0:T(8,128)(2,1)} %copy-done), custom_call_target="tpu_custom_call" | custom-call | flops 1610612736 | bytes 5242880 | tf_op jit(solution)/shard_map/pallas_call | solution.py:282
  266.2 6.5 %shard_map.83.refs_2_ = f32[512,384]{1,0:T(8,128)} custom-call(s32[43]{0:T(128)} %dynamic-slice_bitcast_fusion.plan_ref, bf16[4096,2048]{1,0:T(8,128)(2,1)} %bitcast.19, bf16[2,384,2048]{2,1,0:T(8,128)(2,1)} %split.3.scaled_ref, bf16[1088,384]{1,0:T(8,128)(2,1)} %copy-done.2, bf16[544,384]{1,0:T(8,128)(2,1)} %copy-done.14), custom_call_target="tpu_custom_call" | custom-call | flops 1610612736 | bytes 5242880 | tf_op jit(solution)/shard_map/pallas_call | solution.py:282
  273.4 4.8 %shard_map.87.refs_8_ = f32[1,8,384]{2,1,0:T(8,128)} custom-call(s32[43]{0:T(128)} %dynamic-slice_bitcast_fusion.plan_ref, bf16[4096,2048]{1,0:T(8,128)(2,1)} %bitcast.12, bf16[2,384,2048]{2,1,0:T(8,128)(2,1)} %split.2.scaled_ref, bf16[544,384]{1,0:T(8,128)(2,1)} %copy-done.4, bf16[272,384]{1,0:T(8,128)(2,1)} %copy-done.16, f32[512,384]{1,0:T(8,128)} %shard_map.83.refs_2_), custom_call_target="tpu_custom_call" | custom-call | flops 805306368 | bytes 4194304 | tf_op jit(solution)/shard_map/pallas_call | solution.py:282
  278.2 2.3 collective-permute-start.36
  281.3 1.7 collective-permute-start.38
  283.0 4.8 %shard_map.84.refs_4_ = f32[1,8,384]{2,1,0:T(8,128)} custom-call(s32[43]{0:T(128)} %dynamic-slice_bitcast_fusion.plan_ref, bf16[4096,2048]{1,0:T(8,128)(2,1)} %bitcast.13, bf16[2,384,2048]{2,1,0:T(8,128)(2,1)} %split.2.scaled_ref, bf16[544,384]{1,0:T(8,128)(2,1)} %copy-done.3, bf16[272,384]{1,0:T(8,128)(2,1)} %copy-done.15, f32[512,384]{1,0:T(8,128)} %shard_map.83.refs_2_), custom_call_target="tpu_custom_call" | custom-call | flops 805306368 | bytes 4194304 | tf_op jit(solution)/shard_map/pallas_call | solution.py:282
  289.2 6.2 %shard_map.77.refs_2_ = f32[512,384]{1,0:T(8,128)} custom-call(s32[43]{0:T(128)} %dynamic-slice_bitcast_fusion.plan_ref, bf16[4096,2048]{1,0:T(8,128)(2,1)} %bitcast.20, bf16[2,384,2048]{2,1,0:T(8,128)(2,1)} %split.3.scaled_ref, bf16[1088,384]{1,0:T(8,128)(2,1)} %copy-done.1, bf16[544,384]{1,0:T(8,128)(2,1)} %copy-done.12), custom_call_target="tpu_custom_call" | custom-call | flops 1610612736 | bytes 5242880 | tf_op jit(solution)/shard_map/pallas_call | solution.py:282
  295.4 1.9 collective-permute-done.11.refs_1_
  298.1 6.3 %shard_map.78.refs_0_ = f32[2,8,384]{2,1,0:T(8,128)} custom-call(s32[43]{0:T(128)} %dynamic-slice_bitcast_fusion.plan_ref, bf16[4096,2048]{1,0:T(8,128)(2,1)} %bitcast.14, bf16[2,384,2048]{2,1,0:T(8,128)(2,1)} %split.2.scaled_ref, bf16[1088,384]{1,0:T(8,128)(2,1)} %copy-done, bf16[544,384]{1,0:T(8,128)(2,1)} %copy-done.13, f32[512,384]{1,0:T(8,128)} %shard_map.77.refs_2_), custom_call_target="tpu_custom_call" | custom-call | flops 1610612736 | bytes 5242880 | tf_op jit(solution)/shard_map/pallas_call | solution.py:282
  304.5 1.9 collective-permute-start.25
  306.4 2.5 collective-permute-start.26
  310.5 3.0 collective-permute-done.32.refs_6_
  (131 shorter events, 34.6 us)
Async XLA Ops:
  0.0 21.8 %collective-permute-start.12 = (bf16[192,2048]{1,0:T(8,128)(2,1)}, bf16[192,2048]{1,0:T(8,128)(2,1)}, u32[]{:S(2)}, u32[]{:S(2)}) collective-permute-start(bf16[192,2048]{1,0:T(8,128)(2,1)} %refs_0_.3), channel_id=1, source_target_pairs={{0,8},{8,0},{16,24},{24,16},{1,9},{9,1},{17,25},{25,17},{2,10},{10... | collective-permute-start | bytes 2359304 | tf_op jit(solution)/shard_map/ppermute | solution.py:347
  3.1 23.5 %collective-permute-start.15 = (bf16[192,2048]{1,0:T(8,128)(2,1)}, bf16[192,2048]{1,0:T(8,128)(2,1)S(1)}, u32[]{:S(2)}, u32[]{:S(2)}) collective-permute-start(bf16[192,2048]{1,0:T(8,128)(2,1)} %refs_0_.3), channel_id=1, source_target_pairs={{0,0},{24,24},{8,16},{16,8},{1,1},{25,25},{9,17},{17,9},{2,2},{26,... | collective-permute-start | bytes 2359304 | tf_op jit(solution)/shard_map/ppermute | solution.py:349
  4.8 33.7 %collective-permute-start = (bf16[192,2048]{1,0:T(8,128)(2,1)}, bf16[192,2048]{1,0:T(8,128)(2,1)S(1)}, u32[]{:S(2)}, u32[]{:S(2)}) collective-permute-start(bf16[192,2048]{1,0:T(8,128)(2,1)} %refs_0_.2), channel_id=1, source_target_pairs={{0,8},{8,0},{16,24},{24,16},{1,9},{9,1},{17,25},{25,17},{2,10},{10... | collective-permute-start | bytes 2359304 | tf_op jit(solution)/shard_map/ppermute | solution.py:347
  21.8 24.8 %collective-permute-start.13 = (bf16[192,2048]{1,0:T(8,128)(2,1)}, bf16[192,2048]{1,0:T(8,128)(2,1)S(1)}, u32[]{:S(2)}, u32[]{:S(2)}) collective-permute-start(bf16[192,2048]{1,0:T(8,128)(2,1)} %collective-permute-done.12.refs_0_), channel_id=1, source_target_pairs={{0,0},{24,24},{8,16},{16,8},{1,1},{25,25},{9,17},{17,9},{2,2},{26,... | collective-permute-start | bytes 2359304 | tf_op jit(solution)/shard_map/ppermute | solution.py:349
  23.5 33.7 %collective-permute-start.3 = (bf16[192,2048]{1,0:T(8,128)(2,1)}, bf16[192,2048]{1,0:T(8,128)(2,1)S(1)}, u32[]{:S(2)}, u32[]{:S(2)}) collective-permute-start(bf16[192,2048]{1,0:T(8,128)(2,1)} %refs_0_.2), channel_id=1, source_target_pairs={{0,0},{24,24},{8,16},{16,8},{1,1},{25,25},{9,17},{17,9},{2,2},{26,... | collective-permute-start | bytes 2359304 | tf_op jit(solution)/shard_map/ppermute | solution.py:349
  26.5 20.1 %copy-start.9 = (bf16[192,2048]{1,0:T(8,128)(2,1)}, bf16[192,2048]{1,0:T(8,128)(2,1)S(1)}, u32[]{:S(2)}) copy-start(bf16[192,2048]{1,0:T(8,128)(2,1)S(1)} %collective-permute-done.15.refs_1_) | copy-start | bytes 2359300
  26.5 50.5 %collective-permute-start.16 = (bf16[192,2048]{1,0:T(8,128)(2,1)S(1)}, bf16[192,2048]{1,0:T(8,128)(2,1)}, u32[]{:S(2)}, u32[]{:S(2)}) collective-permute-start(bf16[192,2048]{1,0:T(8,128)(2,1)S(1)} %collective-permute-done.15.refs_1_), channel_id=1, source_target_pairs={{0,8},{8,0},{16,24},{24,16},{1,9},{9,1},{17,25},{25,17},{2,10},{10... | collective-permute-start | bytes 2359304 | tf_op jit(solution)/shard_map/ppermute | solution.py:347
  38.5 8.1 %copy-start.7 = (bf16[192,2048]{1,0:T(8,128)(2,1)}, bf16[192,2048]{1,0:T(8,128)(2,1)S(1)}, u32[]{:S(2)}) copy-start(bf16[192,2048]{1,0:T(8,128)(2,1)S(1)} %collective-permute-done.refs_0_) | copy-start | bytes 2359300
  38.5 32.9 %collective-permute-start.1 = (bf16[192,2048]{1,0:T(8,128)(2,1)S(1)}, bf16[192,2048]{1,0:T(8,128)(2,1)}, u32[]{:S(2)}, u32[]{:S(2)}) collective-permute-start(bf16[192,2048]{1,0:T(8,128)(2,1)S(1)} %collective-permute-done.refs_0_), channel_id=1, source_target_pairs={{0,0},{24,24},{8,16},{16,8},{1,1},{25,25},{9,17},{17,9},{2,2},{26,... | collective-permute-start | bytes 2359304 | tf_op jit(solution)/shard_map/ppermute | solution.py:349
  46.6 10.6 %copy-start.10 = (bf16[192,2048]{1,0:T(8,128)(2,1)}, bf16[192,2048]{1,0:T(8,128)(2,1)S(1)}, u32[]{:S(2)}) copy-start(bf16[192,2048]{1,0:T(8,128)(2,1)S(1)} %collective-permute-done.13.refs_1_) | copy-start | bytes 2359300
  46.6 38.6 %collective-permute-start.14 = (bf16[192,2048]{1,0:T(8,128)(2,1)S(1)}, bf16[192,2048]{1,0:T(8,128)(2,1)}, u32[]{:S(2)}, u32[]{:S(2)}) collective-permute-start(bf16[192,2048]{1,0:T(8,128)(2,1)S(1)} %collective-permute-done.13.refs_1_), channel_id=1, source_target_pairs={{0,8},{8,0},{16,24},{24,16},{1,9},{9,1},{17,25},{25,17},{2,10},{10... | collective-permute-start | bytes 2359304 | tf_op jit(solution)/shard_map/ppermute | solution.py:347
  57.2 14.2 %copy-start.8 = (bf16[192,2048]{1,0:T(8,128)(2,1)}, bf16[192,2048]{1,0:T(8,128)(2,1)S(1)}, u32[]{:S(2)}) copy-start(bf16[192,2048]{1,0:T(8,128)(2,1)S(1)} %collective-permute-done.3.refs_1_) | copy-start | bytes 2359300
  57.2 46.2 %collective-permute-start.4 = (bf16[192,2048]{1,0:T(8,128)(2,1)S(1)}, bf16[192,2048]{1,0:T(8,128)(2,1)}, u32[]{:S(2)}, u32[]{:S(2)}) collective-permute-start(bf16[192,2048]{1,0:T(8,128)(2,1)S(1)} %collective-permute-done.3.refs_1_), channel_id=1, source_target_pairs={{0,8},{8,0},{16,24},{24,16},{1,9},{9,1},{17,25},{25,17},{2,10},{10... | collective-permute-start | bytes 2359304 | tf_op jit(solution)/shard_map/ppermute | solution.py:347
  71.4 40.3 %collective-permute-start.2 = (bf16[192,2048]{1,0:T(8,128)(2,1)}, bf16[192,2048]{1,0:T(8,128)(2,1)S(1)}, u32[]{:S(2)}, u32[]{:S(2)}) collective-permute-start(bf16[192,2048]{1,0:T(8,128)(2,1)} %collective-permute-done.1.refs_1_), channel_id=1, source_target_pairs={{0,8},{8,0},{16,24},{24,16},{1,9},{9,1},{17,25},{25,17},{2,10},{10... | collective-permute-start | bytes 2359304 | tf_op jit(solution)/shard_map/ppermute | solution.py:347
  93.7 51.3 %collective-permute-start.21 = (bf16[208,2048]{1,0:T(8,128)(2,1)}, bf16[208,2048]{1,0:T(8,128)(2,1)S(1)}, u32[]{:S(2)}, u32[]{:S(2)}) collective-permute-start(bf16[208,2048]{1,0:T(8,128)(2,1)} %get-tuple-element.16), channel_id=1, source_target_pairs={{0,1},{1,0},{2,3},{3,2},{4,5},{5,4},{6,7},{7,6},{8,9},{9,8},{10,11... | collective-permute-start | bytes 2555912 | tf_op jit(solution)/shard_map/ppermute | solution.py:360
  111.7 10.0 %copy-start.35 = (f32[1,2048]{1,0:T(1,128)S(1)}, f32[1,2048]{1,0:T(1,128)}, u32[]{:S(2)}) copy-start(f32[1,2048]{1,0:T(1,128)} %get-tuple-element.14) | copy-start | bytes 24580
  121.1 48.4 %collective-permute-start.9 = (bf16[208,2048]{1,0:T(8,128)(2,1)}, bf16[208,2048]{1,0:T(8,128)(2,1)S(1)}, u32[]{:S(2)}, u32[]{:S(2)}) collective-permute-start(bf16[208,2048]{1,0:T(8,128)(2,1)} %get-tuple-element.13), channel_id=1, source_target_pairs={{0,1},{1,0},{2,3},{3,2},{4,5},{5,4},{6,7},{7,6},{8,9},{9,8},{10,11... | collective-permute-start | bytes 2555912 | tf_op jit(solution)/shard_map/ppermute | solution.py:360
  121.6 17.2 %collective-permute-start.17 = (f32[1,2048]{1,0:T(1,128)S(1)}, f32[1,2048]{1,0:T(1,128)S(1)}, u32[]{:S(2)}, u32[]{:S(2)}) collective-permute-start(f32[1,2048]{1,0:T(1,128)S(1)} %copy-done.35), channel_id=1, source_target_pairs={{0,1},{1,0},{2,3},{3,2},{4,5},{5,4},{6,7},{7,6},{8,9},{9,8},{10,11... | collective-permute-start | bytes 24584 | tf_op jit(solution)/shard_map/ppermute | solution.py:361
  123.1 17.4 %collective-permute-start.5 = (f32[1,2048]{1,0:T(1,128)}, f32[1,2048]{1,0:T(1,128)S(1)}, u32[]{:S(2)}, u32[]{:S(2)}) collective-permute-start(f32[1,2048]{1,0:T(1,128)} %get-tuple-element.11), channel_id=1, source_target_pairs={{0,1},{1,0},{2,3},{3,2},{4,5},{5,4},{6,7},{7,6},{8,9},{9,8},{10,11... | collective-permute-start | bytes 24584 | tf_op jit(solution)/shard_map/ppermute | solution.py:361
  138.9 3.8 %collective-permute-start.18 = (f32[1,2048]{1,0:T(1,128)S(1)}, f32[1,2048]{1,0:T(1,128)S(1)}, u32[]{:S(2)}, u32[]{:S(2)}) collective-permute-start(f32[1,2048]{1,0:T(1,128)S(1)} %add.12.refs_0_), channel_id=1, source_target_pairs={{0,2},{2,4},{4,6},{6,0},{1,3},{3,5},{5,7},{7,1},{8,10},{10,12},{12... | collective-permute-start | bytes 24584 | tf_op jit(solution)/shard_map/ppermute | solution.py:362
  139.0 3.8 %collective-permute-start.19 = (f32[1,2048]{1,0:T(1,128)S(1)}, f32[1,2048]{1,0:T(1,128)S(1)}, u32[]{:S(2)}, u32[]{:S(2)}) collective-permute-start(f32[1,2048]{1,0:T(1,128)S(1)} %add.12.refs_0_), channel_id=1, source_target_pairs={{0,4},{2,6},{4,0},{6,2},{1,5},{3,7},{5,1},{7,3},{8,12},{10,14},{12... | collective-permute-start | bytes 24584 | tf_op jit(solution)/shard_map/ppermute | solution.py:362
  140.6 3.7 %collective-permute-start.20 = (f32[1,2048]{1,0:T(1,128)S(1)}, f32[1,2048]{1,0:T(1,128)S(1)}, u32[]{:S(2)}, u32[]{:S(2)}) collective-permute-start(f32[1,2048]{1,0:T(1,128)S(1)} %add.12.refs_0_), channel_id=1, source_target_pairs={{0,6},{2,0},{4,2},{6,4},{1,7},{3,1},{5,3},{7,5},{8,14},{10,8},{12,... | collective-permute-start | bytes 24584 | tf_op jit(solution)/shard_map/ppermute | solution.py:362
  142.7 16.3 %copy-start.18 = (f32[1,2048]{1,0:T(1,128)}, f32[1,2048]{1,0:T(1,128)S(1)}, u32[]{:S(2)}) copy-start(f32[1,2048]{1,0:T(1,128)S(1)} %add.11.refs_0_) | copy-start | bytes 24580
  142.7 25.2 %collective-permute-start.6 = (f32[1,2048]{1,0:T(1,128)S(1)}, f32[1,2048]{1,0:T(1,128)S(1)}, u32[]{:S(2)}, u32[]{:S(2)}) collective-permute-start(f32[1,2048]{1,0:T(1,128)S(1)} %add.11.refs_0_), channel_id=1, source_target_pairs={{0,2},{2,4},{4,6},{6,0},{1,3},{3,5},{5,7},{7,1},{8,10},{10,12},{12... | collective-permute-start | bytes 24584 | tf_op jit(solution)/shard_map/ppermute | solution.py:362
  142.8 26.7 %collective-permute-start.7 = (f32[1,2048]{1,0:T(1,128)S(1)}, f32[1,2048]{1,0:T(1,128)S(1)}, u32[]{:S(2)}, u32[]{:S(2)}) collective-permute-start(f32[1,2048]{1,0:T(1,128)S(1)} %add.11.refs_0_), channel_id=1, source_target_pairs={{0,4},{2,6},{4,0},{6,2},{1,5},{3,7},{5,1},{7,3},{8,12},{10,14},{12... | collective-permute-start | bytes 24584 | tf_op jit(solution)/shard_map/ppermute | solution.py:362
  144.2 25.3 %collective-permute-start.8 = (f32[1,2048]{1,0:T(1,128)S(1)}, f32[1,2048]{1,0:T(1,128)S(1)}, u32[]{:S(2)}, u32[]{:S(2)}) collective-permute-start(f32[1,2048]{1,0:T(1,128)S(1)} %add.11.refs_0_), channel_id=1, source_target_pairs={{0,6},{2,0},{4,2},{6,4},{1,7},{3,1},{5,3},{7,5},{8,14},{10,8},{12,... | collective-permute-start | bytes 24584 | tf_op jit(solution)/shard_map/ppermute | solution.py:362
  159.0 38.9 %collective-permute-start.29 = (bf16[1088,384]{1,0:T(8,128)(2,1)}, bf16[1088,384]{1,0:T(8,128)(2,1)S(1)}, u32[]{:S(2)}, u32[]{:S(2)}) collective-permute-start(bf16[1088,384]{1,0:T(8,128)(2,1)} %shard_map.81), channel_id=1, source_target_pairs={{0,8},{8,0},{16,24},{24,16},{1,9},{9,1},{17,25},{25,17},{2,10},{10... | collective-permute-start | bytes 2506760 | tf_op jit(solution)/shard_map/ppermute | solution.py:304
  167.9 80.5 %collective-permute-start.22 = (bf16[1088,384]{1,0:T(8,128)(2,1)}, bf16[1088,384]{1,0:T(8,128)(2,1)S(1)}, u32[]{:S(2)}, u32[]{:S(2)}) collective-permute-start(bf16[1088,384]{1,0:T(8,128)(2,1)} %shard_map.75), channel_id=1, source_target_pairs={{0,8},{8,0},{16,24},{24,16},{1,9},{9,1},{17,25},{25,17},{2,10},{10... | collective-permute-start | bytes 2506760 | tf_op jit(solution)/shard_map/ppermute | solution.py:304
  183.5 74.2 %collective-permute-start.10 = (bf16[1088,384]{1,0:T(8,128)(2,1)}, bf16[1088,384]{1,0:T(8,128)(2,1)S(1)}, u32[]{:S(2)}, u32[]{:S(2)}) collective-permute-start(bf16[1088,384]{1,0:T(8,128)(2,1)} %shard_map.73), channel_id=1, source_target_pairs={{0,8},{8,0},{16,24},{24,16},{1,9},{9,1},{17,25},{25,17},{2,10},{10... | collective-permute-start | bytes 2506760 | tf_op jit(solution)/shard_map/ppermute | solution.py:304
  189.9 44.5 %collective-permute-start.34 = (bf16[544,384]{1,0:T(8,128)(2,1)}, bf16[544,384]{1,0:T(8,128)(2,1)S(1)}, u32[]{:S(2)}, u32[]{:S(2)}) collective-permute-start(bf16[544,384]{1,0:T(8,128)(2,1)} %shard_map.85), channel_id=1, source_target_pairs={{0,8},{8,0},{16,24},{24,16},{1,9},{9,1},{17,25},{25,17},{2,10},{10... | collective-permute-start | bytes 1253384 | tf_op jit(solution)/shard_map/ppermute | solution.py:304
  197.4 44.7 %collective-permute-start.27 = (bf16[544,384]{1,0:T(8,128)(2,1)}, bf16[544,384]{1,0:T(8,128)(2,1)S(1)}, u32[]{:S(2)}, u32[]{:S(2)}) collective-permute-start(bf16[544,384]{1,0:T(8,128)(2,1)} %shard_map.79), channel_id=1, source_target_pairs={{0,8},{8,0},{16,24},{24,16},{1,9},{9,1},{17,25},{25,17},{2,10},{10... | collective-permute-start | bytes 1253384 | tf_op jit(solution)/shard_map/ppermute | solution.py:304
  204.9 60.5 %collective-permute-start.30 = (bf16[544,384]{1,0:T(8,128)(2,1)}, bf16[544,384]{1,0:T(8,128)(2,1)S(1)}, u32[]{:S(2)}, u32[]{:S(2)}) collective-permute-start(bf16[544,384]{1,0:T(8,128)(2,1)} %shard_map.82), channel_id=1, source_target_pairs={{0,16},{8,24},{16,0},{24,8},{1,17},{9,25},{17,1},{25,9},{2,18},{10... | collective-permute-start | bytes 1253384 | tf_op jit(solution)/shard_map/ppermute | solution.py:304
  239.9 32.8 %collective-permute-start.35 = (bf16[272,384]{1,0:T(8,128)(2,1)}, bf16[272,384]{1,0:T(8,128)(2,1)S(1)}, u32[]{:S(2)}, u32[]{:S(2)}) collective-permute-start(bf16[272,384]{1,0:T(8,128)(2,1)} %shard_map.86), channel_id=1, source_target_pairs={{0,16},{8,24},{16,0},{24,8},{1,17},{9,25},{17,1},{25,9},{2,18},{10... | collective-permute-start | bytes 626696 | tf_op jit(solution)/shard_map/ppermute | solution.py:304
  247.7 33.6 %collective-permute-start.28 = (bf16[272,384]{1,0:T(8,128)(2,1)}, bf16[272,384]{1,0:T(8,128)(2,1)S(1)}, u32[]{:S(2)}, u32[]{:S(2)}) collective-permute-start(bf16[272,384]{1,0:T(8,128)(2,1)} %shard_map.80), channel_id=1, source_target_pairs={{0,16},{8,24},{16,0},{24,8},{1,17},{9,25},{17,1},{25,9},{2,18},{10... | collective-permute-start | bytes 626696 | tf_op jit(solution)/shard_map/ppermute | solution.py:304
  255.5 32.9 %collective-permute-start.23 = (bf16[544,384]{1,0:T(8,128)(2,1)}, bf16[544,384]{1,0:T(8,128)(2,1)S(1)}, u32[]{:S(2)}, u32[]{:S(2)}) collective-permute-start(bf16[544,384]{1,0:T(8,128)(2,1)} %shard_map.76), channel_id=1, source_target_pairs={{0,16},{8,24},{16,0},{24,8},{1,17},{9,25},{17,1},{25,9},{2,18},{10... | collective-permute-start | bytes 1253384 | tf_op jit(solution)/shard_map/ppermute | solution.py:304
  264.7 32.6 %collective-permute-start.11 = (bf16[544,384]{1,0:T(8,128)(2,1)}, bf16[544,384]{1,0:T(8,128)(2,1)S(1)}, u32[]{:S(2)}, u32[]{:S(2)}) collective-permute-start(bf16[544,384]{1,0:T(8,128)(2,1)} %shard_map.74), channel_id=1, source_target_pairs={{0,16},{8,24},{16,0},{24,8},{1,17},{9,25},{17,1},{25,9},{2,18},{10... | collective-permute-start | bytes 1253384 | tf_op jit(solution)/shard_map/ppermute | solution.py:304
  278.2 26.2 %collective-permute-start.36 = (f32[1,8,384]{2,1,0:T(8,128)}, f32[1,8,384]{2,1,0:T(8,128)S(1)}, u32[]{:S(2)}, u32[]{:S(2)}) collective-permute-start(f32[1,8,384]{2,1,0:T(8,128)} %shard_map.87.refs_8_), channel_id=1, source_target_pairs={{0,8},{8,0},{16,24},{24,16},{1,9},{9,1},{17,25},{25,17},{2,10},{10... | collective-permute-start | bytes 36872 | tf_op jit(solution)/shard_map/ppermute | solution.py:405
  280.6 25.8 %collective-permute-start.37 = (f32[1,8,384]{2,1,0:T(8,128)}, f32[1,8,384]{2,1,0:T(8,128)S(1)}, u32[]{:S(2)}, u32[]{:S(2)}) collective-permute-start(f32[1,8,384]{2,1,0:T(8,128)} %shard_map.87.refs_8_), channel_id=1, source_target_pairs={{0,16},{8,24},{16,0},{24,8},{1,17},{9,25},{17,1},{25,9},{2,18},{10... | collective-permute-start | bytes 36872 | tf_op jit(solution)/shard_map/ppermute | solution.py:405
  281.3 27.6 %collective-permute-start.38 = (f32[1,8,384]{2,1,0:T(8,128)}, f32[1,8,384]{2,1,0:T(8,128)S(1)}, u32[]{:S(2)}, u32[]{:S(2)}) collective-permute-start(f32[1,8,384]{2,1,0:T(8,128)} %shard_map.87.refs_8_), channel_id=1, source_target_pairs={{0,24},{8,16},{16,8},{24,0},{1,25},{9,17},{17,9},{25,1},{2,26},{10... | collective-permute-start | bytes 36872 | tf_op jit(solution)/shard_map/ppermute | solution.py:405
  288.4 20.6 %collective-permute-start.31 = (f32[1,8,384]{2,1,0:T(8,128)}, f32[1,8,384]{2,1,0:T(8,128)S(1)}, u32[]{:S(2)}, u32[]{:S(2)}) collective-permute-start(f32[1,8,384]{2,1,0:T(8,128)} %shard_map.84.refs_4_), channel_id=1, source_target_pairs={{0,8},{8,0},{16,24},{24,16},{1,9},{9,1},{17,25},{25,17},{2,10},{10... | collective-permute-start | bytes 36872 | tf_op jit(solution)/shard_map/ppermute | solution.py:405
  295.4 13.5 %copy-start.17 = (f32[1,8,384]{2,1,0:T(8,128)S(1)}, f32[1,8,384]{2,1,0:T(8,128)}, u32[]{:S(2)}) copy-start(f32[1,8,384]{2,1,0:T(8,128)} %shard_map.84.refs_4_) | copy-start | bytes 36868
  304.5 10.1 %collective-permute-start.24 = (f32[2,8,384]{2,1,0:T(8,128)}, f32[2,8,384]{2,1,0:T(8,128)S(1)}, u32[]{:S(2)}, u32[]{:S(2)}) collective-permute-start(f32[2,8,384]{2,1,0:T(8,128)} %shard_map.78.refs_0_), channel_id=1, source_target_pairs={{0,8},{8,0},{16,24},{24,16},{1,9},{9,1},{17,25},{25,17},{2,10},{10... | collective-permute-start | bytes 73736 | tf_op jit(solution)/shard_map/ppermute | solution.py:405
  304.5 10.1 %copy-start.23 = (f32[1,8,384]{2,1,0:T(8,128)}, f32[1,8,384]{2,1,0:T(8,128)S(1)}, u32[]{:S(2)}) copy-start(f32[1,8,384]{2,1,0:T(8,128)S(1)} %collective-permute-done.36.refs_9_) | copy-start | bytes 36868
  304.5 10.1 %collective-permute-start.25 = (f32[2,8,384]{2,1,0:T(8,128)}, f32[2,8,384]{2,1,0:T(8,128)S(1)}, u32[]{:S(2)}, u32[]{:S(2)}) collective-permute-start(f32[2,8,384]{2,1,0:T(8,128)} %shard_map.78.refs_0_), channel_id=1, source_target_pairs={{0,16},{8,24},{16,0},{24,8},{1,17},{9,25},{17,1},{25,9},{2,18},{10... | collective-permute-start | bytes 73736 | tf_op jit(solution)/shard_map/ppermute | solution.py:405
  306.4 8.2 %copy-start.24 = (f32[1,8,384]{2,1,0:T(8,128)}, f32[1,8,384]{2,1,0:T(8,128)S(1)}, u32[]{:S(2)}) copy-start(f32[1,8,384]{2,1,0:T(8,128)S(1)} %collective-permute-done.37.refs_10_) | copy-start | bytes 36868
  306.4 8.2 %collective-permute-start.26 = (f32[2,8,384]{2,1,0:T(8,128)}, f32[2,8,384]{2,1,0:T(8,128)S(1)}, u32[]{:S(2)}, u32[]{:S(2)}) collective-permute-start(f32[2,8,384]{2,1,0:T(8,128)} %shard_map.78.refs_0_), channel_id=1, source_target_pairs={{0,24},{8,16},{16,8},{24,0},{1,25},{9,17},{17,9},{25,1},{2,26},{10... | collective-permute-start | bytes 73736 | tf_op jit(solution)/shard_map/ppermute | solution.py:405
  308.9 4.7 %collective-permute-start.32 = (f32[1,8,384]{2,1,0:T(8,128)S(1)}, f32[1,8,384]{2,1,0:T(8,128)S(1)}, u32[]{:S(2)}, u32[]{:S(2)}) collective-permute-start(f32[1,8,384]{2,1,0:T(8,128)S(1)} %copy-done.17), channel_id=1, source_target_pairs={{0,16},{8,24},{16,0},{24,8},{1,17},{9,25},{17,1},{25,9},{2,18},{10... | collective-permute-start | bytes 36872 | tf_op jit(solution)/shard_map/ppermute | solution.py:405
  309.0 5.6 %collective-permute-start.33 = (f32[1,8,384]{2,1,0:T(8,128)S(1)}, f32[1,8,384]{2,1,0:T(8,128)S(1)}, u32[]{:S(2)}, u32[]{:S(2)}) collective-permute-start(f32[1,8,384]{2,1,0:T(8,128)S(1)} %copy-done.17), channel_id=1, source_target_pairs={{0,24},{8,16},{16,8},{24,0},{1,25},{9,17},{17,9},{25,1},{2,26},{10... | collective-permute-start | bytes 36872 | tf_op jit(solution)/shard_map/ppermute | solution.py:405
  (27 other events, 41.1 us)
where the time goes:
time: 318 us; the launch traced here: 317 us
  Pallas kernels  168 us (53%)
  waiting for transfers between devices  71.5 us (22%)
  starting transfers between devices  65.1 us (20%)
  local copies, waits for them, and re-layouts  11.9 us (4%)
    pallas_call x15, Pallas kernels, pair_step(): pl.pallas_call(body, out_shape=out_shape, grid_spec=pltpu.PrefetchScalarG...  93.9 us
    pallas_call x8, Pallas kernels, rotate_step(): pl.pallas_call(body, out_shape=out_shape, grid_spec=pltpu.PrefetchScalarG...  63 us
    ppermute x10, waiting for transfers between devices, reduce_pairs(): received = received + [in_hbm(lax.ppermute(code, 'width', pairs))]  30.9 us
    ppermute x6, starting transfers between devices, gather_rotate(): got = [lax.ppermute(send_even, 'width', even)]  26.3 us
    ppermute x6, waiting for transfers between devices, gather_rotate(): got = [lax.ppermute(send_even, 'width', even)]  21.2 us
    ppermute x2, waiting for transfers between devices, scaled_group(): total = total + lax.ppermute(squares, 'query', shifted)  15.2 us
    ppermute x10, starting transfers between devices, reduce_pairs(): received = received + [in_hbm(lax.ppermute(code, 'width', pairs))]  11.4 us
    ppermute x9, starting transfers between devices, compute(): lax.ppermute(own, 'width', [(i, i ^ x) for i in range(width)])  11.2 us
  transfers between devices with their start and end apart: 39, of which 9 were waited for; matrix products, arithmetic and copies ran while one was open for 1% of the time, Pallas kernels for 52%

commit v1 on v0

--- a/solution.py
+++ b/solution.py
@@ -28,13 +28,21 @@
     return [(i, (i + by) % count) for i in range(count)]
 
 
+def far_pairs(count):
+    return [(0, count - 1), (count - 1, 0)] + [(i, i) for i in range(1, count - 1)]
+
+
 def line_sources(width, place):
     got = []
-    for distance in range(1, width):
+    for distance in range(1, max(width - 1, 2) if width > 1 else 1):
         right, left = place + distance, place - distance
-        pair = (right, left) if place % 2 == 0 else (left, right)
-        got += [pair[0]] if distance == width - 1 else list(pair)
-    return [source if 0 <= source < width else None for source in got]
+        got += [right, left] if place % 2 == 0 else [left, right]
+        if distance == 1:
+            if width == 2:
+                got = got[:1]
+            else:
+                got.append(width - 1 if place == 0 else 0 if place == width - 1 else None)
+    return [source if source is not None and 0 <= source < width else None for source in got]
 
 
 def rotate_plan(width, nk):
@@ -301,7 +309,7 @@
         nb //= 2
         code = pair_step(rows, scaled, received, plan, firsts[len(received)], shift, nb, block, "code")
         pairs = [(i, i ^ step) for i in range(width)]
-        received = received + [in_hbm(lax.ppermute(code, "width", pairs))]
+        received = received + [in_vmem(lax.ppermute(code, "width", pairs))]
         step *= 2
     mode = "plain" if other is None else "joined"
     return pair_step(
@@ -333,22 +341,26 @@
     )(plan, *arrays)
 
 
-def in_hbm(x):
-    return pltpu.with_memory_space_constraint(x, pltpu.HBM)
+def in_vmem(x):
+    return pltpu.with_memory_space_constraint(x, pltpu.VMEM)
 
 
 def gather_rotate(own, basis, plan, width):
     even, odd = swap_pairs(width)
-    count = 2 * width - 2
+    count = 1 + len(line_sources(width, 0))
     send_even = send_odd = own
     acc = rotate_step(None, 0, [own], basis, plan, count, width == 1)
-    for distance in range(1, width):
-        last = distance == width - 1
+    done = 1
+    for distance in range(1, max(width - 1, 2) if width > 1 else 1):
         got = [lax.ppermute(send_even, "width", even)]
-        if not last:
+        if width > 2:
             got.append(lax.ppermute(send_odd, "width", odd))
             send_even, send_odd = got[1], got[0]
-        acc = rotate_step(acc, 2 * distance - 1, [in_hbm(x) for x in got], basis, plan, count, last)
+            if distance == 1:
+                got.append(lax.ppermute(own, "width", far_pairs(width)))
+        last = done + len(got) == count
+        acc = rotate_step(acc, done, [in_vmem(x) for x in got], basis, plan, count, last)
+        done += len(got)
     return acc
 
 
@@ -357,7 +369,7 @@
     codes, total = [], squares
     for by in range(1, query_count):
         shifted = shift_pairs(query_count, by)
-        codes.append(in_hbm(lax.ppermute(code, "query", shifted)))
+        codes.append(in_vmem(lax.ppermute(code, "query", shifted)))
         total = total + lax.ppermute(squares, "query", shifted)
     sums = [total] + [lax.ppermute(total, "token", shift_pairs(token_count, by)) for by in range(1, token_count)]
     return split_scaled(rotated, codes, sums, place, total_tokens)
@@ -401,10 +413,10 @@
         own = reduce_pairs(
             members, rows_out, scaled_out, plan, firsts[len(members)], block, width, found[members[0]], rank_count
         )
-        batches.append(
-            [own] + [lax.ppermute(own, "width", [(i, i ^ x) for i in range(width)]) for x in range(1, width)]
-        )
-    scores = assemble(batches, plan, parts_at)
+        batches.append(own)
+    own = jnp.concatenate(batches, axis=0)
+    far = [lax.ppermute(own, "width", [(i, i ^ x) for i in range(width)]) for x in range(1, width)]
+    scores = assemble([[own] + far], plan, parts_at)
     return scores.reshape(queries, scores.shape[-1])
 
 

time: 318 us -> 317 us (level)
  starting transfers between devices: 65.1 us -> 76.1 us
  Pallas kernels: 168 us -> 160 us
  local copies, waits for them, and re-layouts: 11.9 us -> 5.26 us
    ppermute x6 -> x4, waiting for transfers between devices: 21.2 us -> 0.01 us  [gather_rotate(): got = [lax.ppermute(send_even, 'width', even)]]
    ppermute x12 -> x14, waiting for transfers between devices: 31 us -> 50.7 us  [the longest x10 43.4 us: reduce_pairs(): received = received + [in_vmem(lax.ppermute(code, 'width', pairs))]]
    ppermute x4, starting transfers between devices: 6.89 us -> 18.2 us  [gather_rotate(): got.append(lax.ppermute(send_odd, 'width', odd))]
    ppermute x12 -> x14, starting transfers between devices: 13.4 us -> 20.3 us  [the longest x10 9.91 us: reduce_pairs(): received = received + [in_vmem(lax.ppermute(code, 'width', pairs))]]
    ppermute x9 -> x3, starting transfers between devices: 11.2 us -> 4.38 us  [compute(): lax.ppermute(own, 'width', [(i, i ^ x) for i in range(width)])]
    pallas_call x8 -> x6, Pallas kernels: 63 us -> 56.2 us  [rotate_step(): pl.pallas_call(body, out_shape=out_shape, grid_spec=pltpu.PrefetchScalarG...]
    unnamed x72 -> x38, local copies, waits for them, and re-layouts: 10.7 us -> 3.99 us
    ppermute x6 -> x4, starting transfers between devices: 26.3 us -> 25.9 us  [gather_rotate(): got = [lax.ppermute(send_even, 'width', even)]]
  transfers between devices with their start and end apart: 39 -> 33, of which waited for: 9 -> 10; matrix products, arithmetic and copies ran while one was open for 1% -> 1% of each run, Pallas kernels for 52% -> 48%
where the time goes in v1:
time: 317 us; the launch traced here: 315 us
  Pallas kernels  160 us (50%)
  starting transfers between devices  76.1 us (24%)
  waiting for transfers between devices  72 us (23%)
  local copies, waits for them, and re-layouts  5.26 us (2%)
    pallas_call x15, Pallas kernels, pair_step(): pl.pallas_call(body, out_shape=out_shape, grid_spec=pltpu.PrefetchScalarG...  93.1 us
    pallas_call x6, Pallas kernels, rotate_step(): pl.pallas_call(body, out_shape=out_shape, grid_spec=pltpu.PrefetchScalarG...  56.2 us
    ppermute x10, waiting for transfers between devices, reduce_pairs(): received = received + [in_vmem(lax.ppermute(code, 'width', pairs))]  43.4 us
    ppermute x4, starting transfers between devices, gather_rotate(): got = [lax.ppermute(send_even, 'width', even)]  25.9 us
    ppermute x4, starting transfers between devices, gather_rotate(): got.append(lax.ppermute(send_odd, 'width', odd))  18.2 us
    ppermute x2, waiting for transfers between devices, scaled_group(): total = total + lax.ppermute(squares, 'query', shifted)  16.8 us
    ppermute x10, starting transfers between devices, reduce_pairs(): received = received + [in_vmem(lax.ppermute(code, 'width', pairs))]  9.91 us
    pallas_call x2, Pallas kernels, split_scaled(): pl.pallas_call(body, out_shape=jax.ShapeDtypeStruct((2, n * tokens, cols)...  8.99 us
  transfers between devices with their start and end apart: 33, of which 10 were waited for; matrix products, arithmetic and copies ran while one was open for 1% of the time, Pallas kernels for 48%

profile of v1, /device:TPU:0, one launch (start us, length us, event | category | flops | bytes accessed | tf_op | source)
XLA Modules:
  0.0 315.0 jit_solution(11221297403113569329)
XLA Ops:
  0.0 1.8 collective-permute-start.12
  1.8 4.8 %collective-permute-start.14 = (bf16[192,2048]{1,0:T(8,128)(2,1)}, bf16[192,2048]{1,0:T(8,128)(2,1)S(1)}, u32[]{:S(2)}, u32[]{:S(2)}) collective-permute-start(bf16[192,2048]{1,0:T(8,128)(2,1)} %refs_0_.3), channel_id=1, source_target_pairs={{0,8},{8,0},{16,24},{24,16},{1,9},{9,1},{17,25},{25,17},{2,10},{10... | collective-permute-start | bytes 2359304 | tf_op jit(solution)/shard_map/ppermute | solution.py:355
  6.6 3.2 %collective-permute-start.16 = (bf16[192,2048]{1,0:T(8,128)(2,1)}, bf16[192,2048]{1,0:T(8,128)(2,1)S(1)}, u32[]{:S(2)}, u32[]{:S(2)}) collective-permute-start(bf16[192,2048]{1,0:T(8,128)(2,1)} %refs_0_.3), channel_id=1, source_target_pairs={{0,24},{24,0},{8,8},{16,16},{1,25},{25,1},{9,9},{17,17},{2,26},{26... | collective-permute-start | bytes 2359304 | tf_op jit(solution)/shard_map/ppermute | solution.py:360
  9.9 7.4 %collective-permute-start = (bf16[192,2048]{1,0:T(8,128)(2,1)}, bf16[192,2048]{1,0:T(8,128)(2,1)}, u32[]{:S(2)}, u32[]{:S(2)}) collective-permute-start(bf16[192,2048]{1,0:T(8,128)(2,1)} %refs_0_.2), channel_id=1, source_target_pairs={{0,0},{24,24},{8,16},{16,8},{1,1},{25,25},{9,17},{17,9},{2,2},{26,... | collective-permute-start | bytes 2359304 | tf_op jit(solution)/shard_map/ppermute | solution.py:357
  17.3 9.5 %collective-permute-start.13 = (bf16[192,2048]{1,0:T(8,128)(2,1)S(1)}, bf16[192,2048]{1,0:T(8,128)(2,1)S(1)}, u32[]{:S(2)}, u32[]{:S(2)}) collective-permute-start(bf16[192,2048]{1,0:T(8,128)(2,1)S(1)} %collective-permute-done.12.refs_1_), channel_id=1, source_target_pairs={{0,8},{8,0},{16,24},{24,16},{1,9},{9,1},{17,25},{25,17},{2,10},{10... | collective-permute-start | bytes 2359304 | tf_op jit(solution)/shard_map/ppermute | solution.py:355
  26.8 1.5 collective-permute-start.15
  29.6 6.5 %rotate.9.refs_5_ = f32[192,2048]{1,0:T(8,128)} custom-call(s32[43]{0:T(128)} %dynamic-slice_bitcast_fusion.plan_ref, bf16[192,2048]{1,0:T(8,128)(2,1)} %refs_0_.3, bf16[8192,2048]{1,0:T(8,128)(2,1)} %refs_3_.7, bf16[8192,2048]{1,0:T(8,128)(2,1)} %refs_3_.7), custom_call_target="tpu_custom_call" | custom-call | flops 3221225472 | bytes 19922944 | tf_op jit(solution)/shard_map/rotate/pallas_call | solution.py:136
  36.2 7.3 %collective-permute-done.16.refs_2_ = bf16[192,2048]{1,0:T(8,128)(2,1)S(1)} collective-permute-done((bf16[192,2048]{1,0:T(8,128)(2,1)}, bf16[192,2048]{1,0:T(8,128)(2,1)S(1)}, u32[]{:S(2)}, u32[]{:S(2)}) %collective-permute-start.16) | collective-permute-done | bytes 786464 | tf_op jit(solution)/shard_map/ppermute | solution.py:360
  43.4 4.4 %collective-permute-start.4 = (bf16[192,2048]{1,0:T(8,128)(2,1)}, bf16[192,2048]{1,0:T(8,128)(2,1)}, u32[]{:S(2)}, u32[]{:S(2)}) collective-permute-start(bf16[192,2048]{1,0:T(8,128)(2,1)} %refs_0_.2), channel_id=1, source_target_pairs={{0,24},{24,0},{8,8},{16,16},{1,25},{25,1},{9,9},{17,17},{2,26},{26... | collective-permute-start | bytes 2359304 | tf_op jit(solution)/shard_map/ppermute | solution.py:360
  47.8 11.5 %collective-permute-start.1 = (bf16[192,2048]{1,0:T(8,128)(2,1)}, bf16[192,2048]{1,0:T(8,128)(2,1)}, u32[]{:S(2)}, u32[]{:S(2)}) collective-permute-start(bf16[192,2048]{1,0:T(8,128)(2,1)} %collective-permute-done.refs_1_), channel_id=1, source_target_pairs={{0,8},{8,0},{16,24},{24,16},{1,9},{9,1},{17,25},{25,17},{2,10},{10... | collective-permute-start | bytes 2359304 | tf_op jit(solution)/shard_map/ppermute | solution.py:355
  59.4 7.4 %collective-permute-start.3 = (bf16[192,2048]{1,0:T(8,128)(2,1)}, bf16[192,2048]{1,0:T(8,128)(2,1)}, u32[]{:S(2)}, u32[]{:S(2)}) collective-permute-start(bf16[192,2048]{1,0:T(8,128)(2,1)} %collective-permute-done.2.refs_0_), channel_id=1, source_target_pairs={{0,0},{24,24},{8,16},{16,8},{1,1},{25,25},{9,17},{17,9},{2,2},{26,... | collective-permute-start | bytes 2359304 | tf_op jit(solution)/shard_map/ppermute | solution.py:357
  66.8 11.7 %rotate.10.refs_4_ = f32[192,2048]{1,0:T(8,128)} custom-call(s32[43]{0:T(128)} %dynamic-slice_bitcast_fusion.plan_ref, bf16[192,2048]{1,0:T(8,128)(2,1)S(1)} %collective-permute-done.14.refs_0_, bf16[192,2048]{1,0:T(8,128)(2,1)S(1)} %collective-permute-done.12.refs_1_, bf16[192,2048]{1,0:T(8,128)(2,1)S(1)} %collective-permute-done.16.refs_2_, ...), custom_call_target="tpu_custom_call" | custom-call | flops 3221225472 | bytes 19922944 | tf_op jit(solution)/shard_map/rotate/pallas_call | solution.py:136
  78.6 9.2 %rotate.11 = (f32[192,2048]{1,0:T(8,128)}, f32[1,2048]{1,0:T(1,128)}, bf16[208,2048]{1,0:T(8,128)(2,1)}) custom-call(s32[43]{0:T(128)} %dynamic-slice_bitcast_fusion.plan_ref, bf16[192,2048]{1,0:T(8,128)(2,1)S(1)} %collective-permute-done.13.refs_0_, bf16[192,2048]{1,0:T(8,128)(2,1)} %collective-permute-done.15.refs_1_, bf16[8192,2048]{1,0:T(8,128)(2,1)} %refs_3_.7, ...), custom_call_target="tpu_custom_call" | custom-call | flops 3221225472 | bytes 19922944 | tf_op jit(solution)/shard_map/rotate/pallas_call | solution.py:136
  87.7 1.5 collective-permute-start.21
  89.2 6.6 %rotate.6.refs_5_ = f32[192,2048]{1,0:T(8,128)} custom-call(s32[43]{0:T(128)} %dynamic-slice_bitcast_fusion.plan_ref, bf16[192,2048]{1,0:T(8,128)(2,1)} %refs_0_.2, bf16[8192,2048]{1,0:T(8,128)(2,1)} %refs_3_.5, bf16[8192,2048]{1,0:T(8,128)(2,1)} %refs_3_.5), custom_call_target="tpu_custom_call" | custom-call | flops 3221225472 | bytes 19922944 | tf_op jit(solution)/shard_map/rotate/pallas_call | solution.py:136
  95.8 12.8 %rotate.7.refs_4_ = f32[192,2048]{1,0:T(8,128)} custom-call(s32[43]{0:T(128)} %dynamic-slice_bitcast_fusion.plan_ref, bf16[192,2048]{1,0:T(8,128)(2,1)} %collective-permute-done.2.refs_0_, bf16[192,2048]{1,0:T(8,128)(2,1)} %collective-permute-done.refs_1_, bf16[192,2048]{1,0:T(8,128)(2,1)} %collective-permute-done.4.refs_2_, bf16[8192,2048]{1,0:T(8,128)(2,1)} %refs_3_.5, ...), custom_call_target="tpu_custom_call" | custom-call | flops 3221225472 | bytes 19922944 | tf_op jit(solution)/shard_map/rotate/pallas_call | solution.py:136
  108.6 9.4 %rotate.8 = (f32[192,2048]{1,0:T(8,128)}, f32[1,2048]{1,0:T(1,128)}, bf16[208,2048]{1,0:T(8,128)(2,1)}) custom-call(s32[43]{0:T(128)} %dynamic-slice_bitcast_fusion.plan_ref, bf16[192,2048]{1,0:T(8,128)(2,1)} %collective-permute-done.1.refs_0_, bf16[192,2048]{1,0:T(8,128)(2,1)} %collective-permute-done.3.refs_1_, bf16[8192,2048]{1,0:T(8,128)(2,1)} %refs_3_.5, ...), custom_call_target="tpu_custom_call" | custom-call | flops 3221225472 | bytes 19922944 | tf_op jit(solution)/shard_map/rotate/pallas_call | solution.py:136
  121.4 16.8 %collective-permute-done.17 = f32[1,2048]{1,0:T(1,128)S(1)} collective-permute-done((f32[1,2048]{1,0:T(1,128)S(1)}, f32[1,2048]{1,0:T(1,128)S(1)}, u32[]{:S(2)}, u32[]{:S(2)}) %collective-permute-start.17) | collective-permute-done | bytes 8224 | tf_op jit(solution)/shard_map/ppermute | solution.py:373
  138.2 1.6 collective-permute-start.19
  144.3 4.5 %split.3.scaled_ref = bf16[2,384,2048]{2,1,0:T(8,128)(2,1)} custom-call(s32[1]{0:T(128)} %bitcast.2.place_ref, f32[1,2048]{1,0:T(1,128)} %copy-done.11, f32[1,2048]{1,0:T(1,128)} %copy-done.13, f32[1,2048]{1,0:T(1,128)} %copy-done.15, f32[1,2048]{1,0:T(1,128)} %copy-done.17, f32[192,2048]{1,0:T(8,128)} %get-tuple-element.15.refs_4_, ...), custom_call_target="tpu_custom_call" | custom-call | flops 6291456 | bytes 6291456 | tf_op jit(solution)/shard_map/split/pallas_call | solution.py:196
  148.9 8.4 %shard_map.81 = bf16[1088,384]{1,0:T(8,128)(2,1)} custom-call(s32[43]{0:T(128)} %dynamic-slice_bitcast_fusion.plan_ref, bf16[4096,2048]{1,0:T(8,128)(2,1)} %bitcast.15, bf16[2,384,2048]{2,1,0:T(8,128)(2,1)} %split.3.scaled_ref), custom_call_target="tpu_custom_call" | custom-call | flops 3221225472 | bytes 7340032 | tf_op jit(solution)/shard_map/pallas_call | solution.py:290
  157.3 2.9 collective-permute-start.26
  160.2 8.5 %shard_map.75 = bf16[1088,384]{1,0:T(8,128)(2,1)} custom-call(s32[43]{0:T(128)} %dynamic-slice_bitcast_fusion.plan_ref, bf16[4096,2048]{1,0:T(8,128)(2,1)} %bitcast.16, bf16[2,384,2048]{2,1,0:T(8,128)(2,1)} %split.3.scaled_ref), custom_call_target="tpu_custom_call" | custom-call | flops 3221225472 | bytes 7340032 | tf_op jit(solution)/shard_map/pallas_call | solution.py:290
  169.3 4.5 %split.2.scaled_ref = bf16[2,384,2048]{2,1,0:T(8,128)(2,1)} custom-call(s32[1]{0:T(128)} %bitcast.2.place_ref, f32[1,2048]{1,0:T(1,128)} %copy-done.10, f32[1,2048]{1,0:T(1,128)} %copy-done.12, f32[1,2048]{1,0:T(1,128)} %copy-done.14, f32[1,2048]{1,0:T(1,128)} %copy-done.16, f32[192,2048]{1,0:T(8,128)} %get-tuple-element.12.refs_4_, ...), custom_call_target="tpu_custom_call" | custom-call | flops 6291456 | bytes 6291456 | tf_op jit(solution)/shard_map/split/pallas_call | solution.py:196
  173.8 8.4 %shard_map.73 = bf16[1088,384]{1,0:T(8,128)(2,1)} custom-call(s32[43]{0:T(128)} %dynamic-slice_bitcast_fusion.plan_ref, bf16[4096,2048]{1,0:T(8,128)(2,1)} %bitcast.6, bf16[2,384,2048]{2,1,0:T(8,128)(2,1)} %split.2.scaled_ref), custom_call_target="tpu_custom_call" | custom-call | flops 3221225472 | bytes 7340032 | tf_op jit(solution)/shard_map/pallas_call | solution.py:290
  182.2 2.0 collective-permute-start.10
  184.2 6.0 %shard_map.79 = bf16[544,384]{1,0:T(8,128)(2,1)} custom-call(s32[43]{0:T(128)} %dynamic-slice_bitcast_fusion.plan_ref, bf16[4096,2048]{1,0:T(8,128)(2,1)} %bitcast.7, bf16[2,384,2048]{2,1,0:T(8,128)(2,1)} %split.2.scaled_ref), custom_call_target="tpu_custom_call" | custom-call | flops 1610612736 | bytes 5242880 | tf_op jit(solution)/shard_map/pallas_call | solution.py:290
  190.2 6.0 %shard_map.85 = bf16[544,384]{1,0:T(8,128)(2,1)} custom-call(s32[43]{0:T(128)} %dynamic-slice_bitcast_fusion.plan_ref, bf16[4096,2048]{1,0:T(8,128)(2,1)} %bitcast.8, bf16[2,384,2048]{2,1,0:T(8,128)(2,1)} %split.2.scaled_ref), custom_call_target="tpu_custom_call" | custom-call | flops 1610612736 | bytes 5242880 | tf_op jit(solution)/shard_map/pallas_call | solution.py:290
  196.2 2.0 collective-permute-start.28
  198.2 6.2 %shard_map.82 = bf16[544,384]{1,0:T(8,128)(2,1)} custom-call(s32[43]{0:T(128)} %dynamic-slice_bitcast_fusion.plan_ref, bf16[4096,2048]{1,0:T(8,128)(2,1)} %bitcast.17, bf16[2,384,2048]{2,1,0:T(8,128)(2,1)} %split.3.scaled_ref, bf16[1088,384]{1,0:T(8,128)(2,1)} %collective-permute-done.26.refs_0_), custom_call_target="tpu_custom_call" | custom-call | flops 1610612736 | bytes 5242880 | tf_op jit(solution)/shard_map/pallas_call | solution.py:290
  204.3 29.3 %collective-permute-done.24.refs_0_ = bf16[544,384]{1,0:T(8,128)(2,1)S(1)} collective-permute-done((bf16[544,384]{1,0:T(8,128)(2,1)}, bf16[544,384]{1,0:T(8,128)(2,1)S(1)}, u32[]{:S(2)}, u32[]{:S(2)}) %collective-permute-start.24) | collective-permute-done | bytes 417824 | tf_op jit(solution)/shard_map/ppermute | solution.py:312
  233.6 4.7 %shard_map.80 = bf16[272,384]{1,0:T(8,128)(2,1)} custom-call(s32[43]{0:T(128)} %dynamic-slice_bitcast_fusion.plan_ref, bf16[4096,2048]{1,0:T(8,128)(2,1)} %bitcast.9, bf16[2,384,2048]{2,1,0:T(8,128)(2,1)} %split.2.scaled_ref, bf16[544,384]{1,0:T(8,128)(2,1)S(1)} %collective-permute-done.24.refs_0_), custom_call_target="tpu_custom_call" | custom-call | flops 805306368 | bytes 4194304 | tf_op jit(solution)/shard_map/pallas_call | solution.py:290
  238.4 3.7 %collective-permute-done.28.refs_0_ = bf16[544,384]{1,0:T(8,128)(2,1)S(1)} collective-permute-done((bf16[544,384]{1,0:T(8,128)(2,1)}, bf16[544,384]{1,0:T(8,128)(2,1)S(1)}, u32[]{:S(2)}, u32[]{:S(2)}) %collective-permute-start.28) | collective-permute-done | bytes 417824 | tf_op jit(solution)/shard_map/ppermute | solution.py:312
  242.1 4.7 %shard_map.86 = bf16[272,384]{1,0:T(8,128)(2,1)} custom-call(s32[43]{0:T(128)} %dynamic-slice_bitcast_fusion.plan_ref, bf16[4096,2048]{1,0:T(8,128)(2,1)} %bitcast.10, bf16[2,384,2048]{2,1,0:T(8,128)(2,1)} %split.2.scaled_ref, bf16[544,384]{1,0:T(8,128)(2,1)S(1)} %collective-permute-done.28.refs_0_), custom_call_target="tpu_custom_call" | custom-call | flops 805306368 | bytes 4194304 | tf_op jit(solution)/shard_map/pallas_call | solution.py:290
  246.8 6.0 %shard_map.76 = bf16[544,384]{1,0:T(8,128)(2,1)} custom-call(s32[43]{0:T(128)} %dynamic-slice_bitcast_fusion.plan_ref, bf16[4096,2048]{1,0:T(8,128)(2,1)} %bitcast.18, bf16[2,384,2048]{2,1,0:T(8,128)(2,1)} %split.3.scaled_ref, bf16[1088,384]{1,0:T(8,128)(2,1)S(1)} %collective-permute-done.22.refs_0_), custom_call_target="tpu_custom_call" | custom-call | flops 1610612736 | bytes 5242880 | tf_op jit(solution)/shard_map/pallas_call | solution.py:290
  252.9 2.9 collective-permute-start.23
  255.8 6.1 %shard_map.74 = bf16[544,384]{1,0:T(8,128)(2,1)} custom-call(s32[43]{0:T(128)} %dynamic-slice_bitcast_fusion.plan_ref, bf16[4096,2048]{1,0:T(8,128)(2,1)} %bitcast.11, bf16[2,384,2048]{2,1,0:T(8,128)(2,1)} %split.2.scaled_ref, bf16[1088,384]{1,0:T(8,128)(2,1)S(1)} %collective-permute-done.10.refs_0_), custom_call_target="tpu_custom_call" | custom-call | flops 1610612736 | bytes 5242880 | tf_op jit(solution)/shard_map/pallas_call | solution.py:290
  263.7 6.3 %shard_map.83.refs_2_ = f32[512,384]{1,0:T(8,128)} custom-call(s32[43]{0:T(128)} %dynamic-slice_bitcast_fusion.plan_ref, bf16[4096,2048]{1,0:T(8,128)(2,1)} %bitcast.19, bf16[2,384,2048]{2,1,0:T(8,128)(2,1)} %split.3.scaled_ref, bf16[1088,384]{1,0:T(8,128)(2,1)} %collective-permute-done.26.refs_0_, bf16[544,384]{1,0:T(8,128)(2,1)S(1)} %copy-done.3), custom_call_target="tpu_custom_call" | custom-call | flops 1610612736 | bytes 5242880 | tf_op jit(solution)/shard_map/pallas_call | solution.py:290
  270.9 4.7 %shard_map.84 = f32[1,8,384]{2,1,0:T(8,128)} custom-call(s32[43]{0:T(128)} %dynamic-slice_bitcast_fusion.plan_ref, bf16[4096,2048]{1,0:T(8,128)(2,1)} %bitcast.12, bf16[2,384,2048]{2,1,0:T(8,128)(2,1)} %split.2.scaled_ref, bf16[544,384]{1,0:T(8,128)(2,1)S(1)} %copy-done.1, bf16[272,384]{1,0:T(8,128)(2,1)S(1)} %collective-permute-done.25.refs_1_, ...), custom_call_target="tpu_custom_call" | custom-call | flops 805306368 | bytes 4194304 | tf_op jit(solution)/shard_map/pallas_call | solution.py:290
  275.7 3.4 %collective-permute-done.29.refs_1_ = bf16[272,384]{1,0:T(8,128)(2,1)} collective-permute-done((bf16[272,384]{1,0:T(8,128)(2,1)}, bf16[272,384]{1,0:T(8,128)(2,1)}, u32[]{:S(2)}, u32[]{:S(2)}) %collective-permute-start.29) | collective-permute-done | bytes 208928 | tf_op jit(solution)/shard_map/ppermute | solution.py:312
  279.1 4.8 %shard_map.87 = f32[1,8,384]{2,1,0:T(8,128)} custom-call(s32[43]{0:T(128)} %dynamic-slice_bitcast_fusion.plan_ref, bf16[4096,2048]{1,0:T(8,128)(2,1)} %bitcast.13, bf16[2,384,2048]{2,1,0:T(8,128)(2,1)} %split.2.scaled_ref, bf16[544,384]{1,0:T(8,128)(2,1)S(1)} %collective-permute-done.28.refs_0_, bf16[272,384]{1,0:T(8,128)(2,1)} %collective-permute-done.29.refs_1_, ...), custom_call_target="tpu_custom_call" | custom-call | flops 805306368 | bytes 4194304 | tf_op jit(solution)/shard_map/pallas_call | solution.py:290
  283.9 4.2 %collective-permute-done.23.refs_1_ = bf16[544,384]{1,0:T(8,128)(2,1)} collective-permute-done((bf16[544,384]{1,0:T(8,128)(2,1)}, bf16[544,384]{1,0:T(8,128)(2,1)}, u32[]{:S(2)}, u32[]{:S(2)}) %collective-permute-start.23) | collective-permute-done | bytes 417824 | tf_op jit(solution)/shard_map/ppermute | solution.py:312
  288.0 6.1 %shard_map.77.refs_2_ = f32[512,384]{1,0:T(8,128)} custom-call(s32[43]{0:T(128)} %dynamic-slice_bitcast_fusion.plan_ref, bf16[4096,2048]{1,0:T(8,128)(2,1)} %bitcast.20, bf16[2,384,2048]{2,1,0:T(8,128)(2,1)} %split.3.scaled_ref, bf16[1088,384]{1,0:T(8,128)(2,1)S(1)} %collective-permute-done.22.refs_0_, bf16[544,384]{1,0:T(8,128)(2,1)} %collective-permute-done.23.refs_1_), custom_call_target="tpu_custom_call" | custom-call | flops 1610612736 | bytes 5242880 | tf_op jit(solution)/shard_map/pallas_call | solution.py:290
  294.1 2.8 collective-permute-done.11.refs_1_
  296.9 6.3 %shard_map.78 = f32[2,8,384]{2,1,0:T(8,128)} custom-call(s32[43]{0:T(128)} %dynamic-slice_bitcast_fusion.plan_ref, bf16[4096,2048]{1,0:T(8,128)(2,1)} %bitcast.14, bf16[2,384,2048]{2,1,0:T(8,128)(2,1)} %split.2.scaled_ref, bf16[1088,384]{1,0:T(8,128)(2,1)S(1)} %collective-permute-done.10.refs_0_, bf16[544,384]{1,0:T(8,128)(2,1)} %collective-permute-done.11.refs_1_, ...), custom_call_target="tpu_custom_call" | custom-call | flops 1610612736 | bytes 5242880 | tf_op jit(solution)/shard_map/pallas_call | solution.py:290
  303.9 3.0 collective-permute-start.31
  309.9 3.0 collective-permute-done.32.refs_3_
  313.5 1.6 assemble.1
  (84 shorter events, 16.8 us)
Async XLA Ops:
  0.0 17.3 %collective-permute-start.12 = (bf16[192,2048]{1,0:T(8,128)(2,1)}, bf16[192,2048]{1,0:T(8,128)(2,1)S(1)}, u32[]{:S(2)}, u32[]{:S(2)}) collective-permute-start(bf16[192,2048]{1,0:T(8,128)(2,1)} %refs_0_.3), channel_id=1, source_target_pairs={{0,0},{24,24},{8,16},{16,8},{1,1},{25,25},{9,17},{17,9},{2,2},{26,... | collective-permute-start | bytes 2359304 | tf_op jit(solution)/shard_map/ppermute | solution.py:357
  1.8 25.0 %collective-permute-start.14 = (bf16[192,2048]{1,0:T(8,128)(2,1)}, bf16[192,2048]{1,0:T(8,128)(2,1)S(1)}, u32[]{:S(2)}, u32[]{:S(2)}) collective-permute-start(bf16[192,2048]{1,0:T(8,128)(2,1)} %refs_0_.3), channel_id=1, source_target_pairs={{0,8},{8,0},{16,24},{24,16},{1,9},{9,1},{17,25},{25,17},{2,10},{10... | collective-permute-start | bytes 2359304 | tf_op jit(solution)/shard_map/ppermute | solution.py:355
  6.6 36.8 %collective-permute-start.16 = (bf16[192,2048]{1,0:T(8,128)(2,1)}, bf16[192,2048]{1,0:T(8,128)(2,1)S(1)}, u32[]{:S(2)}, u32[]{:S(2)}) collective-permute-start(bf16[192,2048]{1,0:T(8,128)(2,1)} %refs_0_.3), channel_id=1, source_target_pairs={{0,24},{24,0},{8,8},{16,16},{1,25},{25,1},{9,9},{17,17},{2,26},{26... | collective-permute-start | bytes 2359304 | tf_op jit(solution)/shard_map/ppermute | solution.py:360
  9.9 38.0 %collective-permute-start = (bf16[192,2048]{1,0:T(8,128)(2,1)}, bf16[192,2048]{1,0:T(8,128)(2,1)}, u32[]{:S(2)}, u32[]{:S(2)}) collective-permute-start(bf16[192,2048]{1,0:T(8,128)(2,1)} %refs_0_.2), channel_id=1, source_target_pairs={{0,0},{24,24},{8,16},{16,8},{1,1},{25,25},{9,17},{17,9},{2,2},{26,... | collective-permute-start | bytes 2359304 | tf_op jit(solution)/shard_map/ppermute | solution.py:357
  17.3 42.1 %collective-permute-start.2 = (bf16[192,2048]{1,0:T(8,128)(2,1)}, bf16[192,2048]{1,0:T(8,128)(2,1)}, u32[]{:S(2)}, u32[]{:S(2)}) collective-permute-start(bf16[192,2048]{1,0:T(8,128)(2,1)} %refs_0_.2), channel_id=1, source_target_pairs={{0,8},{8,0},{16,24},{24,16},{1,9},{9,1},{17,25},{25,17},{2,10},{10... | collective-permute-start | bytes 2359304 | tf_op jit(solution)/shard_map/ppermute | solution.py:355
  17.3 61.3 %collective-permute-start.13 = (bf16[192,2048]{1,0:T(8,128)(2,1)S(1)}, bf16[192,2048]{1,0:T(8,128)(2,1)S(1)}, u32[]{:S(2)}, u32[]{:S(2)}) collective-permute-start(bf16[192,2048]{1,0:T(8,128)(2,1)S(1)} %collective-permute-done.12.refs_1_), channel_id=1, source_target_pairs={{0,8},{8,0},{16,24},{24,16},{1,9},{9,1},{17,25},{25,17},{2,10},{10... | collective-permute-start | bytes 2359304 | tf_op jit(solution)/shard_map/ppermute | solution.py:355
  26.8 51.7 %collective-permute-start.15 = (bf16[192,2048]{1,0:T(8,128)(2,1)S(1)}, bf16[192,2048]{1,0:T(8,128)(2,1)}, u32[]{:S(2)}, u32[]{:S(2)}) collective-permute-start(bf16[192,2048]{1,0:T(8,128)(2,1)S(1)} %collective-permute-done.14.refs_0_), channel_id=1, source_target_pairs={{0,0},{24,24},{8,16},{16,8},{1,1},{25,25},{9,17},{17,9},{2,2},{26,... | collective-permute-start | bytes 2359304 | tf_op jit(solution)/shard_map/ppermute | solution.py:357
  43.4 52.3 %collective-permute-start.4 = (bf16[192,2048]{1,0:T(8,128)(2,1)}, bf16[192,2048]{1,0:T(8,128)(2,1)}, u32[]{:S(2)}, u32[]{:S(2)}) collective-permute-start(bf16[192,2048]{1,0:T(8,128)(2,1)} %refs_0_.2), channel_id=1, source_target_pairs={{0,24},{24,0},{8,8},{16,16},{1,25},{25,1},{9,9},{17,17},{2,26},{26... | collective-permute-start | bytes 2359304 | tf_op jit(solution)/shard_map/ppermute | solution.py:360
  47.8 60.8 %collective-permute-start.1 = (bf16[192,2048]{1,0:T(8,128)(2,1)}, bf16[192,2048]{1,0:T(8,128)(2,1)}, u32[]{:S(2)}, u32[]{:S(2)}) collective-permute-start(bf16[192,2048]{1,0:T(8,128)(2,1)} %collective-permute-done.refs_1_), channel_id=1, source_target_pairs={{0,8},{8,0},{16,24},{24,16},{1,9},{9,1},{17,25},{25,17},{2,10},{10... | collective-permute-start | bytes 2359304 | tf_op jit(solution)/shard_map/ppermute | solution.py:355
  59.4 49.3 %collective-permute-start.3 = (bf16[192,2048]{1,0:T(8,128)(2,1)}, bf16[192,2048]{1,0:T(8,128)(2,1)}, u32[]{:S(2)}, u32[]{:S(2)}) collective-permute-start(bf16[192,2048]{1,0:T(8,128)(2,1)} %collective-permute-done.2.refs_0_), channel_id=1, source_target_pairs={{0,0},{24,24},{8,16},{16,8},{1,1},{25,25},{9,17},{17,9},{2,2},{26,... | collective-permute-start | bytes 2359304 | tf_op jit(solution)/shard_map/ppermute | solution.py:357
  87.7 56.6 %collective-permute-start.21 = (bf16[208,2048]{1,0:T(8,128)(2,1)}, bf16[208,2048]{1,0:T(8,128)(2,1)S(1)}, u32[]{:S(2)}, u32[]{:S(2)}) collective-permute-start(bf16[208,2048]{1,0:T(8,128)(2,1)} %get-tuple-element.16), channel_id=1, source_target_pairs={{0,1},{1,0},{2,3},{3,2},{4,5},{5,4},{6,7},{7,6},{8,9},{9,8},{10,11... | collective-permute-start | bytes 2555912 | tf_op jit(solution)/shard_map/ppermute | solution.py:372
  108.6 10.7 %copy-start.18 = (f32[1,2048]{1,0:T(1,128)S(1)}, f32[1,2048]{1,0:T(1,128)}, u32[]{:S(2)}) copy-start(f32[1,2048]{1,0:T(1,128)} %get-tuple-element.14) | copy-start | bytes 24580
  118.0 50.7 %collective-permute-start.9 = (bf16[208,2048]{1,0:T(8,128)(2,1)}, bf16[208,2048]{1,0:T(8,128)(2,1)S(1)}, u32[]{:S(2)}, u32[]{:S(2)}) collective-permute-start(bf16[208,2048]{1,0:T(8,128)(2,1)} %get-tuple-element.13), channel_id=1, source_target_pairs={{0,1},{1,0},{2,3},{3,2},{4,5},{5,4},{6,7},{7,6},{8,9},{9,8},{10,11... | collective-permute-start | bytes 2555912 | tf_op jit(solution)/shard_map/ppermute | solution.py:372
  119.3 18.8 %collective-permute-start.17 = (f32[1,2048]{1,0:T(1,128)S(1)}, f32[1,2048]{1,0:T(1,128)S(1)}, u32[]{:S(2)}, u32[]{:S(2)}) collective-permute-start(f32[1,2048]{1,0:T(1,128)S(1)} %copy-done.18), channel_id=1, source_target_pairs={{0,1},{1,0},{2,3},{3,2},{4,5},{5,4},{6,7},{7,6},{8,9},{9,8},{10,11... | collective-permute-start | bytes 24584 | tf_op jit(solution)/shard_map/ppermute | solution.py:373
  120.1 19.8 %collective-permute-start.5 = (f32[1,2048]{1,0:T(1,128)}, f32[1,2048]{1,0:T(1,128)S(1)}, u32[]{:S(2)}, u32[]{:S(2)}) collective-permute-start(f32[1,2048]{1,0:T(1,128)} %get-tuple-element.11), channel_id=1, source_target_pairs={{0,1},{1,0},{2,3},{3,2},{4,5},{5,4},{6,7},{7,6},{8,9},{9,8},{10,11... | collective-permute-start | bytes 24584 | tf_op jit(solution)/shard_map/ppermute | solution.py:373
  138.2 6.1 %copy-start.11 = (f32[1,2048]{1,0:T(1,128)}, f32[1,2048]{1,0:T(1,128)S(1)}, u32[]{:S(2)}) copy-start(f32[1,2048]{1,0:T(1,128)S(1)} %add.12.refs_0_) | copy-start | bytes 24580
  138.2 3.8 %collective-permute-start.18 = (f32[1,2048]{1,0:T(1,128)S(1)}, f32[1,2048]{1,0:T(1,128)S(1)}, u32[]{:S(2)}, u32[]{:S(2)}) collective-permute-start(f32[1,2048]{1,0:T(1,128)S(1)} %add.12.refs_0_), channel_id=1, source_target_pairs={{0,2},{2,4},{4,6},{6,0},{1,3},{3,5},{5,7},{7,1},{8,10},{10,12},{12... | collective-permute-start | bytes 24584 | tf_op jit(solution)/shard_map/ppermute | solution.py:374
  138.2 3.8 %collective-permute-start.19 = (f32[1,2048]{1,0:T(1,128)S(1)}, f32[1,2048]{1,0:T(1,128)S(1)}, u32[]{:S(2)}, u32[]{:S(2)}) collective-permute-start(f32[1,2048]{1,0:T(1,128)S(1)} %add.12.refs_0_), channel_id=1, source_target_pairs={{0,4},{2,6},{4,0},{6,2},{1,5},{3,7},{5,1},{7,3},{8,12},{10,14},{12... | collective-permute-start | bytes 24584 | tf_op jit(solution)/shard_map/ppermute | solution.py:374
  139.8 3.7 %collective-permute-start.20 = (f32[1,2048]{1,0:T(1,128)S(1)}, f32[1,2048]{1,0:T(1,128)S(1)}, u32[]{:S(2)}, u32[]{:S(2)}) collective-permute-start(f32[1,2048]{1,0:T(1,128)S(1)} %add.12.refs_0_), channel_id=1, source_target_pairs={{0,6},{2,0},{4,2},{6,4},{1,7},{3,1},{5,3},{7,5},{8,14},{10,8},{12,... | collective-permute-start | bytes 24584 | tf_op jit(solution)/shard_map/ppermute | solution.py:374
  141.9 15.4 %copy-start.10 = (f32[1,2048]{1,0:T(1,128)}, f32[1,2048]{1,0:T(1,128)S(1)}, u32[]{:S(2)}) copy-start(f32[1,2048]{1,0:T(1,128)S(1)} %add.11.refs_0_) | copy-start | bytes 24580
  141.9 2.4 copy-start.13
  142.0 26.7 %collective-permute-start.6 = (f32[1,2048]{1,0:T(1,128)S(1)}, f32[1,2048]{1,0:T(1,128)S(1)}, u32[]{:S(2)}, u32[]{:S(2)}) collective-permute-start(f32[1,2048]{1,0:T(1,128)S(1)} %add.11.refs_0_), channel_id=1, source_target_pairs={{0,2},{2,4},{4,6},{6,0},{1,3},{3,5},{5,7},{7,1},{8,10},{10,12},{12... | collective-permute-start | bytes 24584 | tf_op jit(solution)/shard_map/ppermute | solution.py:374
  142.0 2.3 copy-start.15
  142.0 26.7 %collective-permute-start.7 = (f32[1,2048]{1,0:T(1,128)S(1)}, f32[1,2048]{1,0:T(1,128)S(1)}, u32[]{:S(2)}, u32[]{:S(2)}) collective-permute-start(f32[1,2048]{1,0:T(1,128)S(1)} %add.11.refs_0_), channel_id=1, source_target_pairs={{0,4},{2,6},{4,0},{6,2},{1,5},{3,7},{5,1},{7,3},{8,12},{10,14},{12... | collective-permute-start | bytes 24584 | tf_op jit(solution)/shard_map/ppermute | solution.py:374
  143.5 0.8 copy-start.17
  143.5 25.3 %collective-permute-start.8 = (f32[1,2048]{1,0:T(1,128)S(1)}, f32[1,2048]{1,0:T(1,128)S(1)}, u32[]{:S(2)}, u32[]{:S(2)}) collective-permute-start(f32[1,2048]{1,0:T(1,128)S(1)} %add.11.refs_0_), channel_id=1, source_target_pairs={{0,6},{2,0},{4,2},{6,4},{1,7},{3,1},{5,3},{7,5},{8,14},{10,8},{12,... | collective-permute-start | bytes 24584 | tf_op jit(solution)/shard_map/ppermute | solution.py:374
  157.3 40.9 %collective-permute-start.26 = (bf16[1088,384]{1,0:T(8,128)(2,1)}, bf16[1088,384]{1,0:T(8,128)(2,1)}, u32[]{:S(2)}, u32[]{:S(2)}) collective-permute-start(bf16[1088,384]{1,0:T(8,128)(2,1)} %shard_map.81), channel_id=1, source_target_pairs={{0,8},{8,0},{16,24},{24,16},{1,9},{9,1},{17,25},{25,17},{2,10},{10... | collective-permute-start | bytes 2506760 | tf_op jit(solution)/shard_map/ppermute | solution.py:312
  168.7 78.1 %collective-permute-start.22 = (bf16[1088,384]{1,0:T(8,128)(2,1)}, bf16[1088,384]{1,0:T(8,128)(2,1)S(1)}, u32[]{:S(2)}, u32[]{:S(2)}) collective-permute-start(bf16[1088,384]{1,0:T(8,128)(2,1)} %shard_map.75), channel_id=1, source_target_pairs={{0,8},{8,0},{16,24},{24,16},{1,9},{9,1},{17,25},{25,17},{2,10},{10... | collective-permute-start | bytes 2506760 | tf_op jit(solution)/shard_map/ppermute | solution.py:312
  182.2 73.6 %collective-permute-start.10 = (bf16[1088,384]{1,0:T(8,128)(2,1)}, bf16[1088,384]{1,0:T(8,128)(2,1)S(1)}, u32[]{:S(2)}, u32[]{:S(2)}) collective-permute-start(bf16[1088,384]{1,0:T(8,128)(2,1)} %shard_map.73), channel_id=1, source_target_pairs={{0,8},{8,0},{16,24},{24,16},{1,9},{9,1},{17,25},{25,17},{2,10},{10... | collective-permute-start | bytes 2506760 | tf_op jit(solution)/shard_map/ppermute | solution.py:312
  190.2 43.4 %collective-permute-start.24 = (bf16[544,384]{1,0:T(8,128)(2,1)}, bf16[544,384]{1,0:T(8,128)(2,1)S(1)}, u32[]{:S(2)}, u32[]{:S(2)}) collective-permute-start(bf16[544,384]{1,0:T(8,128)(2,1)} %shard_map.79), channel_id=1, source_target_pairs={{0,8},{8,0},{16,24},{24,16},{1,9},{9,1},{17,25},{25,17},{2,10},{10... | collective-permute-start | bytes 1253384 | tf_op jit(solution)/shard_map/ppermute | solution.py:312
  196.2 45.9 %collective-permute-start.28 = (bf16[544,384]{1,0:T(8,128)(2,1)}, bf16[544,384]{1,0:T(8,128)(2,1)S(1)}, u32[]{:S(2)}, u32[]{:S(2)}) collective-permute-start(bf16[544,384]{1,0:T(8,128)(2,1)} %shard_map.85), channel_id=1, source_target_pairs={{0,8},{8,0},{16,24},{24,16},{1,9},{9,1},{17,25},{25,17},{2,10},{10... | collective-permute-start | bytes 1253384 | tf_op jit(solution)/shard_map/ppermute | solution.py:312
  204.3 57.5 %collective-permute-start.27 = (bf16[544,384]{1,0:T(8,128)(2,1)}, bf16[544,384]{1,0:T(8,128)(2,1)S(1)}, u32[]{:S(2)}, u32[]{:S(2)}) collective-permute-start(bf16[544,384]{1,0:T(8,128)(2,1)} %shard_map.82), channel_id=1, source_target_pairs={{0,16},{8,24},{16,0},{24,8},{1,17},{9,25},{17,1},{25,9},{2,18},{10... | collective-permute-start | bytes 1253384 | tf_op jit(solution)/shard_map/ppermute | solution.py:312
  233.6 4.8 %copy-start = (bf16[544,384]{1,0:T(8,128)(2,1)}, bf16[544,384]{1,0:T(8,128)(2,1)S(1)}, u32[]{:S(2)}) copy-start(bf16[544,384]{1,0:T(8,128)(2,1)S(1)} %collective-permute-done.24.refs_0_) | copy-start | bytes 1253380
  238.4 31.6 %collective-permute-start.25 = (bf16[272,384]{1,0:T(8,128)(2,1)}, bf16[272,384]{1,0:T(8,128)(2,1)S(1)}, u32[]{:S(2)}, u32[]{:S(2)}) collective-permute-start(bf16[272,384]{1,0:T(8,128)(2,1)} %shard_map.80), channel_id=1, source_target_pairs={{0,16},{8,24},{16,0},{24,8},{1,17},{9,25},{17,1},{25,9},{2,18},{10... | collective-permute-start | bytes 626696 | tf_op jit(solution)/shard_map/ppermute | solution.py:312
  246.8 32.2 %collective-permute-start.29 = (bf16[272,384]{1,0:T(8,128)(2,1)}, bf16[272,384]{1,0:T(8,128)(2,1)}, u32[]{:S(2)}, u32[]{:S(2)}) collective-permute-start(bf16[272,384]{1,0:T(8,128)(2,1)} %shard_map.86), channel_id=1, source_target_pairs={{0,16},{8,24},{16,0},{24,8},{1,17},{9,25},{17,1},{25,9},{2,18},{10... | collective-permute-start | bytes 626696 | tf_op jit(solution)/shard_map/ppermute | solution.py:312
  252.9 35.1 %collective-permute-start.23 = (bf16[544,384]{1,0:T(8,128)(2,1)}, bf16[544,384]{1,0:T(8,128)(2,1)}, u32[]{:S(2)}, u32[]{:S(2)}) collective-permute-start(bf16[544,384]{1,0:T(8,128)(2,1)} %shard_map.76), channel_id=1, source_target_pairs={{0,16},{8,24},{16,0},{24,8},{1,17},{9,25},{17,1},{25,9},{2,18},{10... | collective-permute-start | bytes 1253384 | tf_op jit(solution)/shard_map/ppermute | solution.py:312
  261.9 35.0 %collective-permute-start.11 = (bf16[544,384]{1,0:T(8,128)(2,1)}, bf16[544,384]{1,0:T(8,128)(2,1)}, u32[]{:S(2)}, u32[]{:S(2)}) collective-permute-start(bf16[544,384]{1,0:T(8,128)(2,1)} %shard_map.74), channel_id=1, source_target_pairs={{0,16},{8,24},{16,0},{24,8},{1,17},{9,25},{17,1},{25,9},{2,18},{10... | collective-permute-start | bytes 1253384 | tf_op jit(solution)/shard_map/ppermute | solution.py:312
  261.9 0.8 copy-start.2
  262.7 1.0 copy-start.3
  269.9 1.0 copy-start.1
  294.1 9.1 %copy-start.8 = (f32[1,8,384]{2,1,0:T(8,128)S(1)}, f32[1,8,384]{2,1,0:T(8,128)}, u32[]{:S(2)}) copy-start(f32[1,8,384]{2,1,0:T(8,128)} %shard_map.84) | copy-start | bytes 36868
  294.1 9.1 %copy-start.9 = (f32[1,8,384]{2,1,0:T(8,128)S(1)}, f32[1,8,384]{2,1,0:T(8,128)}, u32[]{:S(2)}) copy-start(f32[1,8,384]{2,1,0:T(8,128)} %shard_map.87) | copy-start | bytes 36868
  303.9 8.9 %copy-start.4 = (f32[4,8,384]{2,1,0:T(8,128)}, f32[4,8,384]{2,1,0:T(8,128)S(1)}, u32[]{:S(2)}) copy-start(f32[4,8,384]{2,1,0:T(8,128)S(1)} %pad_maximum_fusion.refs_0_) | copy-start | bytes 147460
  303.9 4.8 %collective-permute-start.30 = (f32[4,8,384]{2,1,0:T(8,128)S(1)}, f32[4,8,384]{2,1,0:T(8,128)S(1)}, u32[]{:S(2)}, u32[]{:S(2)}) collective-permute-start(f32[4,8,384]{2,1,0:T(8,128)S(1)} %pad_maximum_fusion.refs_0_), channel_id=1, source_target_pairs={{0,8},{8,0},{16,24},{24,16},{1,9},{9,1},{17,25},{25,17},{2,10},{10... | collective-permute-start | bytes 147464 | tf_op jit(solution)/shard_map/ppermute | solution.py:418
  303.9 6.0 %collective-permute-start.31 = (f32[4,8,384]{2,1,0:T(8,128)S(1)}, f32[4,8,384]{2,1,0:T(8,128)S(1)}, u32[]{:S(2)}, u32[]{:S(2)}) collective-permute-start(f32[4,8,384]{2,1,0:T(8,128)S(1)} %pad_maximum_fusion.refs_0_), channel_id=1, source_target_pairs={{0,16},{8,24},{16,0},{24,8},{1,17},{9,25},{17,1},{25,9},{2,18},{10... | collective-permute-start | bytes 147464 | tf_op jit(solution)/shard_map/ppermute | solution.py:418
  306.9 5.9 %collective-permute-start.32 = (f32[4,8,384]{2,1,0:T(8,128)S(1)}, f32[4,8,384]{2,1,0:T(8,128)S(1)}, u32[]{:S(2)}, u32[]{:S(2)}) collective-permute-start(f32[4,8,384]{2,1,0:T(8,128)S(1)} %pad_maximum_fusion.refs_0_), channel_id=1, source_target_pairs={{0,24},{8,16},{16,8},{24,0},{1,25},{9,17},{17,9},{25,1},{2,26},{10... | collective-permute-start | bytes 147464 | tf_op jit(solution)/shard_map/ppermute | solution.py:418
  308.7 4.1 %copy-start.5 = (f32[4,8,384]{2,1,0:T(8,128)}, f32[4,8,384]{2,1,0:T(8,128)S(1)}, u32[]{:S(2)}) copy-start(f32[4,8,384]{2,1,0:T(8,128)S(1)} %collective-permute-done.30.refs_1_) | copy-start | bytes 147460
  309.9 3.0 copy-start.6
  (4 other events, 2.4 us)

commit v2 on v1

--- a/solution.py
+++ b/solution.py
@@ -13,9 +13,9 @@
 basis_block = 1024
 basis_streams = 2
 split_block = 512
-chunks = 4
-groups_in = ((0, 1), (2, 3))
-groups_out = ((0, 1), (2,), (3,))
+chunks = 2
+groups_in = ((0,), (1,))
+groups_out = ((0,), (1,))
 
 
 def swap_pairs(count):
@@ -37,11 +37,10 @@
     for distance in range(1, max(width - 1, 2) if width > 1 else 1):
         right, left = place + distance, place - distance
         got += [right, left] if place % 2 == 0 else [left, right]
-        if distance == 1:
-            if width == 2:
-                got = got[:1]
-            else:
-                got.append(width - 1 if place == 0 else 0 if place == width - 1 else None)
+    if width == 2:
+        got = got[:1]
+    elif width > 2:
+        got.append(width - 1 if place == 0 else 0 if place == width - 1 else None)
     return [source if source is not None and 0 <= source < width else None for source in got]
 
 
@@ -356,7 +355,7 @@
         if width > 2:
             got.append(lax.ppermute(send_odd, "width", odd))
             send_even, send_odd = got[1], got[0]
-            if distance == 1:
+            if distance == width - 2:
                 got.append(lax.ppermute(own, "width", far_pairs(width)))
         last = done + len(got) == count
         acc = rotate_step(acc, done, [in_vmem(x) for x in got], basis, plan, count, last)

time: 317 us -> 314 us (level)
  waiting for transfers between devices: 72 us -> 85.3 us
  Pallas kernels: 160 us -> 151 us
  starting transfers between devices: 76.1 us -> 72.7 us
    ppermute x4, waiting for transfers between devices: 0.01 us -> 12.2 us  [gather_rotate(): got = [lax.ppermute(send_even, 'width', even)]]
    ppermute x10 -> x8, waiting for transfers between devices: 43.4 us -> 52.5 us  [reduce_pairs(): received = received + [in_vmem(lax.ppermute(code, 'width', pairs))]]
    pallas_call x15 -> x12, Pallas kernels: 93.1 us -> 84.3 us  [pair_step(): pl.pallas_call(body, out_shape=out_shape, grid_spec=pltpu.PrefetchScalarG...]
    ppermute x2, waiting for transfers between devices: 7.29 us -> 0.08 us  [gather_rotate(): got.append(lax.ppermute(own, 'width', far_pairs(width)))]
    ppermute x10 -> x8, starting transfers between devices: 9.91 us -> 6.2 us  [reduce_pairs(): received = received + [in_vmem(lax.ppermute(code, 'width', pairs))]]
  transfers between devices with their start and end apart: 33 -> 31, of which waited for: 10 -> 12; matrix products, arithmetic and copies ran while one was open for 1% -> 1% of each run, Pallas kernels for 48% -> 46%
where the time goes in v2:
time: 314 us; the launch traced here: 313 us
  Pallas kernels  151 us (48%)
  waiting for transfers between devices  85.3 us (27%)
  starting transfers between devices  72.7 us (23%)
    pallas_call x12, Pallas kernels, pair_step(): pl.pallas_call(body, out_shape=out_shape, grid_spec=pltpu.PrefetchScalarG...  84.3 us
    pallas_call x6, Pallas kernels, rotate_step(): pl.pallas_call(body, out_shape=out_shape, grid_spec=pltpu.PrefetchScalarG...  55.6 us
    ppermute x8, waiting for transfers between devices, reduce_pairs(): received = received + [in_vmem(lax.ppermute(code, 'width', pairs))]  52.5 us
    ppermute x4, starting transfers between devices, gather_rotate(): got = [lax.ppermute(send_even, 'width', even)]  25.9 us
    ppermute x4, starting transfers between devices, gather_rotate(): got.append(lax.ppermute(send_odd, 'width', odd))  18.3 us
    ppermute x2, waiting for transfers between devices, scaled_group(): total = total + lax.ppermute(squares, 'query', shifted)  16.8 us
    ppermute x4, waiting for transfers between devices, gather_rotate(): got = [lax.ppermute(send_even, 'width', even)]  12.2 us
    pallas_call x2, Pallas kernels, split_scaled(): pl.pallas_call(body, out_shape=jax.ShapeDtypeStruct((2, n * tokens, cols)...  9.09 us
  transfers between devices with their start and end apart: 31, of which 12 were waited for; matrix products, arithmetic and copies ran while one was open for 1% of the time, Pallas kernels for 46%

profile of v2, /device:TPU:0, one launch (start us, length us, event | category | flops | bytes accessed | tf_op | source)
XLA Modules:
  0.0 312.7 jit_solution(17778679101425399005)
XLA Ops:
  0.0 1.8 collective-permute-start.12
  1.8 4.8 %collective-permute-start.14 = (bf16[192,2048]{1,0:T(8,128)(2,1)}, bf16[192,2048]{1,0:T(8,128)(2,1)S(1)}, u32[]{:S(2)}, u32[]{:S(2)}) collective-permute-start(bf16[192,2048]{1,0:T(8,128)(2,1)} %refs_0_.3), channel_id=1, source_target_pairs={{0,8},{8,0},{16,24},{24,16},{1,9},{9,1},{17,25},{25,17},{2,10},{10... | collective-permute-start | bytes 2359304 | tf_op jit(solution)/shard_map/ppermute | solution.py:354
  6.6 3.2 %collective-permute-start.16 = (bf16[192,2048]{1,0:T(8,128)(2,1)}, bf16[192,2048]{1,0:T(8,128)(2,1)S(1)}, u32[]{:S(2)}, u32[]{:S(2)}) collective-permute-start(bf16[192,2048]{1,0:T(8,128)(2,1)} %refs_0_.3), channel_id=1, source_target_pairs={{0,24},{24,0},{8,8},{16,16},{1,25},{25,1},{9,9},{17,17},{2,26},{26... | collective-permute-start | bytes 2359304 | tf_op jit(solution)/shard_map/ppermute | solution.py:359
  9.9 7.4 %collective-permute-start = (bf16[192,2048]{1,0:T(8,128)(2,1)}, bf16[192,2048]{1,0:T(8,128)(2,1)}, u32[]{:S(2)}, u32[]{:S(2)}) collective-permute-start(bf16[192,2048]{1,0:T(8,128)(2,1)} %refs_0_.2), channel_id=1, source_target_pairs={{0,0},{24,24},{8,16},{16,8},{1,1},{25,25},{9,17},{17,9},{2,2},{26,... | collective-permute-start | bytes 2359304 | tf_op jit(solution)/shard_map/ppermute | solution.py:356
  17.3 9.5 %collective-permute-start.13 = (bf16[192,2048]{1,0:T(8,128)(2,1)S(1)}, bf16[192,2048]{1,0:T(8,128)(2,1)S(1)}, u32[]{:S(2)}, u32[]{:S(2)}) collective-permute-start(bf16[192,2048]{1,0:T(8,128)(2,1)S(1)} %collective-permute-done.12.refs_1_), channel_id=1, source_target_pairs={{0,8},{8,0},{16,24},{24,16},{1,9},{9,1},{17,25},{25,17},{2,10},{10... | collective-permute-start | bytes 2359304 | tf_op jit(solution)/shard_map/ppermute | solution.py:354
  26.8 1.6 collective-permute-start.15
  29.6 6.5 %rotate.9.refs_4_ = f32[192,2048]{1,0:T(8,128)} custom-call(s32[29]{0:T(128)} %dynamic-slice_bitcast_fusion.plan_ref, bf16[192,2048]{1,0:T(8,128)(2,1)} %refs_0_.3, bf16[8192,2048]{1,0:T(8,128)(2,1)} %refs_4_.3, bf16[8192,2048]{1,0:T(8,128)(2,1)} %refs_4_.3), custom_call_target="tpu_custom_call" | custom-call | flops 3221225472 | bytes 19922944 | tf_op jit(solution)/shard_map/rotate/pallas_call | solution.py:135
  36.2 7.2 %rotate.10.refs_5_ = f32[192,2048]{1,0:T(8,128)} custom-call(s32[29]{0:T(128)} %dynamic-slice_bitcast_fusion.plan_ref, bf16[192,2048]{1,0:T(8,128)(2,1)S(1)} %collective-permute-done.14.refs_0_, bf16[192,2048]{1,0:T(8,128)(2,1)S(1)} %collective-permute-done.12.refs_1_, bf16[8192,2048]{1,0:T(8,128)(2,1)} %refs_4_.3, bf16[8192,2048]{1,0:T(8,128)(2,1)} %refs_4_.3, ...), custom_call_target="tpu_custom_call" | custom-call | flops 3221225472 | bytes 19922944 | tf_op jit(solution)/shard_map/rotate/pallas_call | solution.py:135
  43.4 4.4 %collective-permute-start.4 = (bf16[192,2048]{1,0:T(8,128)(2,1)}, bf16[192,2048]{1,0:T(8,128)(2,1)}, u32[]{:S(2)}, u32[]{:S(2)}) collective-permute-start(bf16[192,2048]{1,0:T(8,128)(2,1)} %refs_0_.2), channel_id=1, source_target_pairs={{0,24},{24,0},{8,8},{16,16},{1,25},{25,1},{9,9},{17,17},{2,26},{26... | collective-permute-start | bytes 2359304 | tf_op jit(solution)/shard_map/ppermute | solution.py:359
  47.8 11.5 %collective-permute-start.1 = (bf16[192,2048]{1,0:T(8,128)(2,1)}, bf16[192,2048]{1,0:T(8,128)(2,1)}, u32[]{:S(2)}, u32[]{:S(2)}) collective-permute-start(bf16[192,2048]{1,0:T(8,128)(2,1)} %collective-permute-done.refs_1_), channel_id=1, source_target_pairs={{0,8},{8,0},{16,24},{24,16},{1,9},{9,1},{17,25},{25,17},{2,10},{10... | collective-permute-start | bytes 2359304 | tf_op jit(solution)/shard_map/ppermute | solution.py:354
  59.4 7.4 %collective-permute-start.3 = (bf16[192,2048]{1,0:T(8,128)(2,1)}, bf16[192,2048]{1,0:T(8,128)(2,1)}, u32[]{:S(2)}, u32[]{:S(2)}) collective-permute-start(bf16[192,2048]{1,0:T(8,128)(2,1)} %collective-permute-done.2.refs_0_), channel_id=1, source_target_pairs={{0,0},{24,24},{8,16},{16,8},{1,1},{25,25},{9,17},{17,9},{2,2},{26,... | collective-permute-start | bytes 2359304 | tf_op jit(solution)/shard_map/ppermute | solution.py:356
  66.8 10.4 %collective-permute-done.13.refs_0_ = bf16[192,2048]{1,0:T(8,128)(2,1)S(1)} collective-permute-done((bf16[192,2048]{1,0:T(8,128)(2,1)S(1)}, bf16[192,2048]{1,0:T(8,128)(2,1)S(1)}, u32[]{:S(2)}, u32[]{:S(2)}) %collective-permute-start.13) | collective-permute-done | bytes 786464 | tf_op jit(solution)/shard_map/ppermute | solution.py:354
  77.2 13.1 %rotate.11 = (f32[192,2048]{1,0:T(8,128)}, f32[1,2048]{1,0:T(1,128)}, bf16[208,2048]{1,0:T(8,128)(2,1)}) custom-call(s32[29]{0:T(128)} %dynamic-slice_bitcast_fusion.plan_ref, bf16[192,2048]{1,0:T(8,128)(2,1)S(1)} %collective-permute-done.13.refs_0_, bf16[192,2048]{1,0:T(8,128)(2,1)} %collective-permute-done.15.refs_1_, ...), custom_call_target="tpu_custom_call" | custom-call | flops 3221225472 | bytes 19922944 | tf_op jit(solution)/shard_map/rotate/pallas_call | solution.py:135
  90.3 1.5 collective-permute-start.21
  91.8 6.6 %rotate.6.refs_4_ = f32[192,2048]{1,0:T(8,128)} custom-call(s32[29]{0:T(128)} %dynamic-slice_bitcast_fusion.plan_ref, bf16[192,2048]{1,0:T(8,128)(2,1)} %refs_0_.2, bf16[8192,2048]{1,0:T(8,128)(2,1)} %refs_4_.2, bf16[8192,2048]{1,0:T(8,128)(2,1)} %refs_4_.2), custom_call_target="tpu_custom_call" | custom-call | flops 3221225472 | bytes 19922944 | tf_op jit(solution)/shard_map/rotate/pallas_call | solution.py:135
  98.3 8.2 %rotate.7.refs_5_ = f32[192,2048]{1,0:T(8,128)} custom-call(s32[29]{0:T(128)} %dynamic-slice_bitcast_fusion.plan_ref, bf16[192,2048]{1,0:T(8,128)(2,1)} %collective-permute-done.2.refs_0_, bf16[192,2048]{1,0:T(8,128)(2,1)} %collective-permute-done.refs_1_, bf16[8192,2048]{1,0:T(8,128)(2,1)} %refs_4_.2, bf16[8192,2048]{1,0:T(8,128)(2,1)} %refs_4_.2, ...), custom_call_target="tpu_custom_call" | custom-call | flops 3221225472 | bytes 19922944 | tf_op jit(solution)/shard_map/rotate/pallas_call | solution.py:135
  106.6 1.9 collective-permute-done.1.refs_0_
  108.4 14.0 %rotate.8 = (f32[192,2048]{1,0:T(8,128)}, f32[1,2048]{1,0:T(1,128)}, bf16[208,2048]{1,0:T(8,128)(2,1)}) custom-call(s32[29]{0:T(128)} %dynamic-slice_bitcast_fusion.plan_ref, bf16[192,2048]{1,0:T(8,128)(2,1)} %collective-permute-done.1.refs_0_, bf16[192,2048]{1,0:T(8,128)(2,1)} %collective-permute-done.3.refs_1_, ...), custom_call_target="tpu_custom_call" | custom-call | flops 3221225472 | bytes 19922944 | tf_op jit(solution)/shard_map/rotate/pallas_call | solution.py:135
  122.5 1.5 collective-permute-start.9
  124.5 1.5 collective-permute-start.5
  126.0 16.8 %collective-permute-done.17 = f32[1,2048]{1,0:T(1,128)S(1)} collective-permute-done((f32[1,2048]{1,0:T(1,128)S(1)}, f32[1,2048]{1,0:T(1,128)S(1)}, u32[]{:S(2)}, u32[]{:S(2)}) %collective-permute-start.17) | collective-permute-done | bytes 8224 | tf_op jit(solution)/shard_map/ppermute | solution.py:372
  142.9 1.6 collective-permute-start.19
  146.7 1.4 collective-permute-start.7
  149.0 4.4 %split.3.scaled_ref = bf16[2,384,2048]{2,1,0:T(8,128)(2,1)} custom-call(s32[1]{0:T(128)} %bitcast.2.place_ref, f32[1,2048]{1,0:T(1,128)} %copy-done.8, f32[1,2048]{1,0:T(1,128)} %copy-done.10, f32[1,2048]{1,0:T(1,128)} %copy-done.12, f32[1,2048]{1,0:T(1,128)} %copy-done.14, f32[192,2048]{1,0:T(8,128)} %get-tuple-element.15.refs_4_, ...), custom_call_target="tpu_custom_call" | custom-call | flops 6291456 | bytes 6291456 | tf_op jit(solution)/shard_map/split/pallas_call | solution.py:195
  153.4 8.3 %shard_map.75 = bf16[1056,384]{1,0:T(8,128)(2,1)} custom-call(s32[29]{0:T(128)} %dynamic-slice_bitcast_fusion.plan_ref, bf16[4096,2048]{1,0:T(8,128)(2,1)} %bitcast.6, bf16[2,384,2048]{2,1,0:T(8,128)(2,1)} %split.3.scaled_ref), custom_call_target="tpu_custom_call" | custom-call | flops 3221225472 | bytes 7340032 | tf_op jit(solution)/shard_map/pallas_call | solution.py:289
  161.7 8.3 %shard_map.81 = bf16[1056,384]{1,0:T(8,128)(2,1)} custom-call(s32[29]{0:T(128)} %dynamic-slice_bitcast_fusion.plan_ref, bf16[4096,2048]{1,0:T(8,128)(2,1)} %bitcast.7, bf16[2,384,2048]{2,1,0:T(8,128)(2,1)} %split.3.scaled_ref), custom_call_target="tpu_custom_call" | custom-call | flops 3221225472 | bytes 7340032 | tf_op jit(solution)/shard_map/pallas_call | solution.py:289
  170.0 2.0 collective-permute-start.26
  172.6 4.7 %split.2.scaled_ref = bf16[2,384,2048]{2,1,0:T(8,128)(2,1)} custom-call(s32[1]{0:T(128)} %bitcast.2.place_ref, f32[1,2048]{1,0:T(1,128)} %copy-done.7, f32[1,2048]{1,0:T(1,128)} %copy-done.9, f32[1,2048]{1,0:T(1,128)} %copy-done.11, f32[1,2048]{1,0:T(1,128)} %copy-done.13, f32[192,2048]{1,0:T(8,128)} %get-tuple-element.12.refs_4_, ...), custom_call_target="tpu_custom_call" | custom-call | flops 6291456 | bytes 6291456 | tf_op jit(solution)/shard_map/split/pallas_call | solution.py:195
  177.3 8.3 %shard_map.73 = bf16[1056,384]{1,0:T(8,128)(2,1)} custom-call(s32[29]{0:T(128)} %dynamic-slice_bitcast_fusion.plan_ref, bf16[4096,2048]{1,0:T(8,128)(2,1)} %bitcast.12, bf16[2,384,2048]{2,1,0:T(8,128)(2,1)} %split.2.scaled_ref), custom_call_target="tpu_custom_call" | custom-call | flops 3221225472 | bytes 7340032 | tf_op jit(solution)/shard_map/pallas_call | solution.py:289
  185.7 8.3 %shard_map.79 = bf16[1056,384]{1,0:T(8,128)(2,1)} custom-call(s32[29]{0:T(128)} %dynamic-slice_bitcast_fusion.plan_ref, bf16[4096,2048]{1,0:T(8,128)(2,1)} %bitcast.13, bf16[2,384,2048]{2,1,0:T(8,128)(2,1)} %split.2.scaled_ref), custom_call_target="tpu_custom_call" | custom-call | flops 3221225472 | bytes 7340032 | tf_op jit(solution)/shard_map/pallas_call | solution.py:289
  194.0 1.9 collective-permute-start.24
  196.0 6.3 %shard_map.76 = bf16[528,384]{1,0:T(8,128)(2,1)} custom-call(s32[29]{0:T(128)} %dynamic-slice_bitcast_fusion.plan_ref, bf16[4096,2048]{1,0:T(8,128)(2,1)} %bitcast.8, bf16[2,384,2048]{2,1,0:T(8,128)(2,1)} %split.3.scaled_ref, bf16[1056,384]{1,0:T(8,128)(2,1)S(1)} %collective-permute-done.22.refs_0_), custom_call_target="tpu_custom_call" | custom-call | flops 1610612736 | bytes 5242880 | tf_op jit(solution)/shard_map/pallas_call | solution.py:289
  203.2 14.1 %collective-permute-done.26.refs_0_ = bf16[1056,384]{1,0:T(8,128)(2,1)S(1)} collective-permute-done((bf16[1056,384]{1,0:T(8,128)(2,1)}, bf16[1056,384]{1,0:T(8,128)(2,1)S(1)}, u32[]{:S(2)}, u32[]{:S(2)}) %collective-permute-start.26) | collective-permute-done | bytes 811040 | tf_op jit(solution)/shard_map/ppermute | solution.py:311
  217.2 6.3 %shard_map.82 = bf16[528,384]{1,0:T(8,128)(2,1)} custom-call(s32[29]{0:T(128)} %dynamic-slice_bitcast_fusion.plan_ref, bf16[4096,2048]{1,0:T(8,128)(2,1)} %bitcast.9, bf16[2,384,2048]{2,1,0:T(8,128)(2,1)} %split.3.scaled_ref, bf16[1056,384]{1,0:T(8,128)(2,1)S(1)} %collective-permute-done.26.refs_0_), custom_call_target="tpu_custom_call" | custom-call | flops 1610612736 | bytes 5242880 | tf_op jit(solution)/shard_map/pallas_call | solution.py:289
  224.0 19.3 %collective-permute-done.10.refs_0_ = bf16[1056,384]{1,0:T(8,128)(2,1)S(1)} collective-permute-done((bf16[1056,384]{1,0:T(8,128)(2,1)}, bf16[1056,384]{1,0:T(8,128)(2,1)S(1)}, u32[]{:S(2)}, u32[]{:S(2)}) %collective-permute-start.10) | collective-permute-done | bytes 811040 | tf_op jit(solution)/shard_map/ppermute | solution.py:311
  243.3 6.3 %shard_map.74 = bf16[528,384]{1,0:T(8,128)(2,1)} custom-call(s32[29]{0:T(128)} %dynamic-slice_bitcast_fusion.plan_ref, bf16[4096,2048]{1,0:T(8,128)(2,1)} %bitcast.14, bf16[2,384,2048]{2,1,0:T(8,128)(2,1)} %split.2.scaled_ref, bf16[1056,384]{1,0:T(8,128)(2,1)S(1)} %collective-permute-done.10.refs_0_), custom_call_target="tpu_custom_call" | custom-call | flops 1610612736 | bytes 5242880 | tf_op jit(solution)/shard_map/pallas_call | solution.py:289
  250.1 10.0 %collective-permute-done.24.refs_0_ = bf16[1056,384]{1,0:T(8,128)(2,1)} collective-permute-done((bf16[1056,384]{1,0:T(8,128)(2,1)}, bf16[1056,384]{1,0:T(8,128)(2,1)}, u32[]{:S(2)}, u32[]{:S(2)}) %collective-permute-start.24) | collective-permute-done | bytes 811040 | tf_op jit(solution)/shard_map/ppermute | solution.py:311
  260.0 6.4 %shard_map.80 = bf16[528,384]{1,0:T(8,128)(2,1)} custom-call(s32[29]{0:T(128)} %dynamic-slice_bitcast_fusion.plan_ref, bf16[4096,2048]{1,0:T(8,128)(2,1)} %bitcast.15, bf16[2,384,2048]{2,1,0:T(8,128)(2,1)} %split.2.scaled_ref, bf16[1056,384]{1,0:T(8,128)(2,1)} %collective-permute-done.24.refs_0_), custom_call_target="tpu_custom_call" | custom-call | flops 1610612736 | bytes 5242880 | tf_op jit(solution)/shard_map/pallas_call | solution.py:289
  266.7 6.3 %shard_map.77.refs_2_ = f32[512,384]{1,0:T(8,128)} custom-call(s32[29]{0:T(128)} %dynamic-slice_bitcast_fusion.plan_ref, bf16[4096,2048]{1,0:T(8,128)(2,1)} %bitcast.10, bf16[2,384,2048]{2,1,0:T(8,128)(2,1)} %split.3.scaled_ref, bf16[1056,384]{1,0:T(8,128)(2,1)S(1)} %collective-permute-done.22.refs_0_, bf16[528,384]{1,0:T(8,128)(2,1)S(1)} %collective-permute-done.23.refs_1_), custom_call_target="tpu_custom_call" | custom-call | flops 1610612736 | bytes 5242880 | tf_op jit(solution)/shard_map/pallas_call | solution.py:289
  273.0 6.8 %shard_map.83.refs_2_ = f32[512,384]{1,0:T(8,128)} custom-call(s32[29]{0:T(128)} %dynamic-slice_bitcast_fusion.plan_ref, bf16[4096,2048]{1,0:T(8,128)(2,1)} %bitcast.11, bf16[2,384,2048]{2,1,0:T(8,128)(2,1)} %split.3.scaled_ref, bf16[1056,384]{1,0:T(8,128)(2,1)S(1)} %collective-permute-done.26.refs_0_, bf16[528,384]{1,0:T(8,128)(2,1)} %collective-permute-done.27.refs_1_), custom_call_target="tpu_custom_call" | custom-call | flops 1610612736 | bytes 5242880 | tf_op jit(solution)/shard_map/pallas_call | solution.py:289
  279.8 6.7 %collective-permute-done.11.refs_1_ = bf16[528,384]{1,0:T(8,128)(2,1)S(1)} collective-permute-done((bf16[528,384]{1,0:T(8,128)(2,1)}, bf16[528,384]{1,0:T(8,128)(2,1)S(1)}, u32[]{:S(2)}, u32[]{:S(2)}) %collective-permute-start.11) | collective-permute-done | bytes 405536 | tf_op jit(solution)/shard_map/ppermute | solution.py:311
  286.5 6.3 %shard_map.78 = f32[1,16,384]{2,1,0:T(8,128)} custom-call(s32[29]{0:T(128)} %dynamic-slice_bitcast_fusion.plan_ref, bf16[4096,2048]{1,0:T(8,128)(2,1)} %bitcast.16, bf16[2,384,2048]{2,1,0:T(8,128)(2,1)} %split.2.scaled_ref, bf16[1056,384]{1,0:T(8,128)(2,1)S(1)} %copy-done.1, bf16[528,384]{1,0:T(8,128)(2,1)S(1)} %collective-permute-done.11.refs_1_, ...), custom_call_target="tpu_custom_call" | custom-call | flops 1610612736 | bytes 5242880 | tf_op jit(solution)/shard_map/pallas_call | solution.py:289
  292.8 2.4 collective-permute-done.25.refs_1_
  295.2 6.5 %shard_map.84 = f32[1,16,384]{2,1,0:T(8,128)} custom-call(s32[29]{0:T(128)} %dynamic-slice_bitcast_fusion.plan_ref, bf16[4096,2048]{1,0:T(8,128)(2,1)} %bitcast.17, bf16[2,384,2048]{2,1,0:T(8,128)(2,1)} %split.2.scaled_ref, bf16[1056,384]{1,0:T(8,128)(2,1)} %collective-permute-done.24.refs_0_, bf16[528,384]{1,0:T(8,128)(2,1)} %collective-permute-done.25.refs_1_, ...), custom_call_target="tpu_custom_call" | custom-call | flops 1610612736 | bytes 5242880 | tf_op jit(solution)/shard_map/pallas_call | solution.py:289
  302.5 2.2 collective-permute-start.29
  304.6 2.2 collective-permute-start.30
  308.1 2.4 collective-permute-done.30.refs_3_
  311.1 1.6 assemble.1
  (71 shorter events, 10.4 us)
Async XLA Ops:
  0.0 17.3 %collective-permute-start.12 = (bf16[192,2048]{1,0:T(8,128)(2,1)}, bf16[192,2048]{1,0:T(8,128)(2,1)S(1)}, u32[]{:S(2)}, u32[]{:S(2)}) collective-permute-start(bf16[192,2048]{1,0:T(8,128)(2,1)} %refs_0_.3), channel_id=1, source_target_pairs={{0,0},{24,24},{8,16},{16,8},{1,1},{25,25},{9,17},{17,9},{2,2},{26,... | collective-permute-start | bytes 2359304 | tf_op jit(solution)/shard_map/ppermute | solution.py:356
  1.8 25.0 %collective-permute-start.14 = (bf16[192,2048]{1,0:T(8,128)(2,1)}, bf16[192,2048]{1,0:T(8,128)(2,1)S(1)}, u32[]{:S(2)}, u32[]{:S(2)}) collective-permute-start(bf16[192,2048]{1,0:T(8,128)(2,1)} %refs_0_.3), channel_id=1, source_target_pairs={{0,8},{8,0},{16,24},{24,16},{1,9},{9,1},{17,25},{25,17},{2,10},{10... | collective-permute-start | bytes 2359304 | tf_op jit(solution)/shard_map/ppermute | solution.py:354
  6.6 36.8 %collective-permute-start.16 = (bf16[192,2048]{1,0:T(8,128)(2,1)}, bf16[192,2048]{1,0:T(8,128)(2,1)S(1)}, u32[]{:S(2)}, u32[]{:S(2)}) collective-permute-start(bf16[192,2048]{1,0:T(8,128)(2,1)} %refs_0_.3), channel_id=1, source_target_pairs={{0,24},{24,0},{8,8},{16,16},{1,25},{25,1},{9,9},{17,17},{2,26},{26... | collective-permute-start | bytes 2359304 | tf_op jit(solution)/shard_map/ppermute | solution.py:359
  9.9 38.0 %collective-permute-start = (bf16[192,2048]{1,0:T(8,128)(2,1)}, bf16[192,2048]{1,0:T(8,128)(2,1)}, u32[]{:S(2)}, u32[]{:S(2)}) collective-permute-start(bf16[192,2048]{1,0:T(8,128)(2,1)} %refs_0_.2), channel_id=1, source_target_pairs={{0,0},{24,24},{8,16},{16,8},{1,1},{25,25},{9,17},{17,9},{2,2},{26,... | collective-permute-start | bytes 2359304 | tf_op jit(solution)/shard_map/ppermute | solution.py:356
  17.3 42.1 %collective-permute-start.2 = (bf16[192,2048]{1,0:T(8,128)(2,1)}, bf16[192,2048]{1,0:T(8,128)(2,1)}, u32[]{:S(2)}, u32[]{:S(2)}) collective-permute-start(bf16[192,2048]{1,0:T(8,128)(2,1)} %refs_0_.2), channel_id=1, source_target_pairs={{0,8},{8,0},{16,24},{24,16},{1,9},{9,1},{17,25},{25,17},{2,10},{10... | collective-permute-start | bytes 2359304 | tf_op jit(solution)/shard_map/ppermute | solution.py:354
  17.3 59.9 %collective-permute-start.13 = (bf16[192,2048]{1,0:T(8,128)(2,1)S(1)}, bf16[192,2048]{1,0:T(8,128)(2,1)S(1)}, u32[]{:S(2)}, u32[]{:S(2)}) collective-permute-start(bf16[192,2048]{1,0:T(8,128)(2,1)S(1)} %collective-permute-done.12.refs_1_), channel_id=1, source_target_pairs={{0,8},{8,0},{16,24},{24,16},{1,9},{9,1},{17,25},{25,17},{2,10},{10... | collective-permute-start | bytes 2359304 | tf_op jit(solution)/shard_map/ppermute | solution.py:354
  26.8 50.4 %collective-permute-start.15 = (bf16[192,2048]{1,0:T(8,128)(2,1)S(1)}, bf16[192,2048]{1,0:T(8,128)(2,1)}, u32[]{:S(2)}, u32[]{:S(2)}) collective-permute-start(bf16[192,2048]{1,0:T(8,128)(2,1)S(1)} %collective-permute-done.14.refs_0_), channel_id=1, source_target_pairs={{0,0},{24,24},{8,16},{16,8},{1,1},{25,25},{9,17},{17,9},{2,2},{26,... | collective-permute-start | bytes 2359304 | tf_op jit(solution)/shard_map/ppermute | solution.py:356
  43.4 63.1 %collective-permute-start.4 = (bf16[192,2048]{1,0:T(8,128)(2,1)}, bf16[192,2048]{1,0:T(8,128)(2,1)}, u32[]{:S(2)}, u32[]{:S(2)}) collective-permute-start(bf16[192,2048]{1,0:T(8,128)(2,1)} %refs_0_.2), channel_id=1, source_target_pairs={{0,24},{24,0},{8,8},{16,16},{1,25},{25,1},{9,9},{17,17},{2,26},{26... | collective-permute-start | bytes 2359304 | tf_op jit(solution)/shard_map/ppermute | solution.py:359
  47.8 60.6 %collective-permute-start.1 = (bf16[192,2048]{1,0:T(8,128)(2,1)}, bf16[192,2048]{1,0:T(8,128)(2,1)}, u32[]{:S(2)}, u32[]{:S(2)}) collective-permute-start(bf16[192,2048]{1,0:T(8,128)(2,1)} %collective-permute-done.refs_1_), channel_id=1, source_target_pairs={{0,8},{8,0},{16,24},{24,16},{1,9},{9,1},{17,25},{25,17},{2,10},{10... | collective-permute-start | bytes 2359304 | tf_op jit(solution)/shard_map/ppermute | solution.py:354
  59.4 49.1 %collective-permute-start.3 = (bf16[192,2048]{1,0:T(8,128)(2,1)}, bf16[192,2048]{1,0:T(8,128)(2,1)}, u32[]{:S(2)}, u32[]{:S(2)}) collective-permute-start(bf16[192,2048]{1,0:T(8,128)(2,1)} %collective-permute-done.2.refs_0_), channel_id=1, source_target_pairs={{0,0},{24,24},{8,16},{16,8},{1,1},{25,25},{9,17},{17,9},{2,2},{26,... | collective-permute-start | bytes 2359304 | tf_op jit(solution)/shard_map/ppermute | solution.py:356
  90.3 58.7 %collective-permute-start.21 = (bf16[208,2048]{1,0:T(8,128)(2,1)}, bf16[208,2048]{1,0:T(8,128)(2,1)S(1)}, u32[]{:S(2)}, u32[]{:S(2)}) collective-permute-start(bf16[208,2048]{1,0:T(8,128)(2,1)} %get-tuple-element.16), channel_id=1, source_target_pairs={{0,1},{1,0},{2,3},{3,2},{4,5},{5,4},{6,7},{7,6},{8,9},{9,8},{10,11... | collective-permute-start | bytes 2555912 | tf_op jit(solution)/shard_map/ppermute | solution.py:371
  106.6 17.4 %copy-start.15 = (f32[1,2048]{1,0:T(1,128)S(1)}, f32[1,2048]{1,0:T(1,128)}, u32[]{:S(2)}) copy-start(f32[1,2048]{1,0:T(1,128)} %get-tuple-element.14) | copy-start | bytes 24580
  122.5 49.6 %collective-permute-start.9 = (bf16[208,2048]{1,0:T(8,128)(2,1)}, bf16[208,2048]{1,0:T(8,128)(2,1)}, u32[]{:S(2)}, u32[]{:S(2)}) collective-permute-start(bf16[208,2048]{1,0:T(8,128)(2,1)} %get-tuple-element.13), channel_id=1, source_target_pairs={{0,1},{1,0},{2,3},{3,2},{4,5},{5,4},{6,7},{7,6},{8,9},{9,8},{10,11... | collective-permute-start | bytes 2555912 | tf_op jit(solution)/shard_map/ppermute | solution.py:371
  124.0 18.8 %collective-permute-start.17 = (f32[1,2048]{1,0:T(1,128)S(1)}, f32[1,2048]{1,0:T(1,128)S(1)}, u32[]{:S(2)}, u32[]{:S(2)}) collective-permute-start(f32[1,2048]{1,0:T(1,128)S(1)} %copy-done.15), channel_id=1, source_target_pairs={{0,1},{1,0},{2,3},{3,2},{4,5},{5,4},{6,7},{7,6},{8,9},{9,8},{10,11... | collective-permute-start | bytes 24584 | tf_op jit(solution)/shard_map/ppermute | solution.py:372
  124.5 20.0 %collective-permute-start.5 = (f32[1,2048]{1,0:T(1,128)}, f32[1,2048]{1,0:T(1,128)S(1)}, u32[]{:S(2)}, u32[]{:S(2)}) collective-permute-start(f32[1,2048]{1,0:T(1,128)} %get-tuple-element.11), channel_id=1, source_target_pairs={{0,1},{1,0},{2,3},{3,2},{4,5},{5,4},{6,7},{7,6},{8,9},{9,8},{10,11... | collective-permute-start | bytes 24584 | tf_op jit(solution)/shard_map/ppermute | solution.py:372
  142.8 6.1 %copy-start.8 = (f32[1,2048]{1,0:T(1,128)}, f32[1,2048]{1,0:T(1,128)S(1)}, u32[]{:S(2)}) copy-start(f32[1,2048]{1,0:T(1,128)S(1)} %add.12.refs_0_) | copy-start | bytes 24580
  142.8 3.8 %collective-permute-start.18 = (f32[1,2048]{1,0:T(1,128)S(1)}, f32[1,2048]{1,0:T(1,128)S(1)}, u32[]{:S(2)}, u32[]{:S(2)}) collective-permute-start(f32[1,2048]{1,0:T(1,128)S(1)} %add.12.refs_0_), channel_id=1, source_target_pairs={{0,2},{2,4},{4,6},{6,0},{1,3},{3,5},{5,7},{7,1},{8,10},{10,12},{12... | collective-permute-start | bytes 24584 | tf_op jit(solution)/shard_map/ppermute | solution.py:373
  142.9 3.8 %collective-permute-start.19 = (f32[1,2048]{1,0:T(1,128)S(1)}, f32[1,2048]{1,0:T(1,128)S(1)}, u32[]{:S(2)}, u32[]{:S(2)}) collective-permute-start(f32[1,2048]{1,0:T(1,128)S(1)} %add.12.refs_0_), channel_id=1, source_target_pairs={{0,4},{2,6},{4,0},{6,2},{1,5},{3,7},{5,1},{7,3},{8,12},{10,14},{12... | collective-permute-start | bytes 24584 | tf_op jit(solution)/shard_map/ppermute | solution.py:373
  144.5 3.7 %collective-permute-start.20 = (f32[1,2048]{1,0:T(1,128)S(1)}, f32[1,2048]{1,0:T(1,128)S(1)}, u32[]{:S(2)}, u32[]{:S(2)}) collective-permute-start(f32[1,2048]{1,0:T(1,128)S(1)} %add.12.refs_0_), channel_id=1, source_target_pairs={{0,6},{2,0},{4,2},{6,4},{1,7},{3,1},{5,3},{7,5},{8,14},{10,8},{12,... | collective-permute-start | bytes 24584 | tf_op jit(solution)/shard_map/ppermute | solution.py:373
  146.6 15.1 %copy-start.7 = (f32[1,2048]{1,0:T(1,128)}, f32[1,2048]{1,0:T(1,128)S(1)}, u32[]{:S(2)}) copy-start(f32[1,2048]{1,0:T(1,128)S(1)} %add.11.refs_0_) | copy-start | bytes 24580
  146.6 2.4 copy-start.10
  146.6 23.4 %collective-permute-start.6 = (f32[1,2048]{1,0:T(1,128)S(1)}, f32[1,2048]{1,0:T(1,128)S(1)}, u32[]{:S(2)}, u32[]{:S(2)}) collective-permute-start(f32[1,2048]{1,0:T(1,128)S(1)} %add.11.refs_0_), channel_id=1, source_target_pairs={{0,2},{2,4},{4,6},{6,0},{1,3},{3,5},{5,7},{7,1},{8,10},{10,12},{12... | collective-permute-start | bytes 24584 | tf_op jit(solution)/shard_map/ppermute | solution.py:373
  146.7 2.3 copy-start.12
  146.7 25.4 %collective-permute-start.7 = (f32[1,2048]{1,0:T(1,128)S(1)}, f32[1,2048]{1,0:T(1,128)S(1)}, u32[]{:S(2)}, u32[]{:S(2)}) collective-permute-start(f32[1,2048]{1,0:T(1,128)S(1)} %add.11.refs_0_), channel_id=1, source_target_pairs={{0,4},{2,6},{4,0},{6,2},{1,5},{3,7},{5,1},{7,3},{8,12},{10,14},{12... | collective-permute-start | bytes 24584 | tf_op jit(solution)/shard_map/ppermute | solution.py:373
  148.1 0.8 copy-start.14
  148.1 23.9 %collective-permute-start.8 = (f32[1,2048]{1,0:T(1,128)S(1)}, f32[1,2048]{1,0:T(1,128)S(1)}, u32[]{:S(2)}, u32[]{:S(2)}) collective-permute-start(f32[1,2048]{1,0:T(1,128)S(1)} %add.11.refs_0_), channel_id=1, source_target_pairs={{0,6},{2,0},{4,2},{6,4},{1,7},{3,1},{5,3},{7,5},{8,14},{10,8},{12,... | collective-permute-start | bytes 24584 | tf_op jit(solution)/shard_map/ppermute | solution.py:373
  170.0 25.9 %collective-permute-start.22 = (bf16[1056,384]{1,0:T(8,128)(2,1)}, bf16[1056,384]{1,0:T(8,128)(2,1)S(1)}, u32[]{:S(2)}, u32[]{:S(2)}) collective-permute-start(bf16[1056,384]{1,0:T(8,128)(2,1)} %shard_map.75), channel_id=1, source_target_pairs={{0,8},{8,0},{16,24},{24,16},{1,9},{9,1},{17,25},{25,17},{2,10},{10... | collective-permute-start | bytes 2433032 | tf_op jit(solution)/shard_map/ppermute | solution.py:311
  170.0 2.1 copy-start.9
  170.0 47.2 %collective-permute-start.26 = (bf16[1056,384]{1,0:T(8,128)(2,1)}, bf16[1056,384]{1,0:T(8,128)(2,1)S(1)}, u32[]{:S(2)}, u32[]{:S(2)}) collective-permute-start(bf16[1056,384]{1,0:T(8,128)(2,1)} %shard_map.81), channel_id=1, source_target_pairs={{0,8},{8,0},{16,24},{24,16},{1,9},{9,1},{17,25},{25,17},{2,10},{10... | collective-permute-start | bytes 2433032 | tf_op jit(solution)/shard_map/ppermute | solution.py:311
  172.0 0.6 copy-start.11
  172.1 0.6 copy-start.13
  185.6 57.7 %collective-permute-start.10 = (bf16[1056,384]{1,0:T(8,128)(2,1)}, bf16[1056,384]{1,0:T(8,128)(2,1)S(1)}, u32[]{:S(2)}, u32[]{:S(2)}) collective-permute-start(bf16[1056,384]{1,0:T(8,128)(2,1)} %shard_map.73), channel_id=1, source_target_pairs={{0,8},{8,0},{16,24},{24,16},{1,9},{9,1},{17,25},{25,17},{2,10},{10... | collective-permute-start | bytes 2433032 | tf_op jit(solution)/shard_map/ppermute | solution.py:311
  194.0 66.0 %collective-permute-start.24 = (bf16[1056,384]{1,0:T(8,128)(2,1)}, bf16[1056,384]{1,0:T(8,128)(2,1)}, u32[]{:S(2)}, u32[]{:S(2)}) collective-permute-start(bf16[1056,384]{1,0:T(8,128)(2,1)} %shard_map.79), channel_id=1, source_target_pairs={{0,8},{8,0},{16,24},{24,16},{1,9},{9,1},{17,25},{25,17},{2,10},{10... | collective-permute-start | bytes 2433032 | tf_op jit(solution)/shard_map/ppermute | solution.py:311
  202.3 64.5 %collective-permute-start.23 = (bf16[528,384]{1,0:T(8,128)(2,1)}, bf16[528,384]{1,0:T(8,128)(2,1)S(1)}, u32[]{:S(2)}, u32[]{:S(2)}) collective-permute-start(bf16[528,384]{1,0:T(8,128)(2,1)} %shard_map.76), channel_id=1, source_target_pairs={{0,16},{8,24},{16,0},{24,8},{1,17},{9,25},{17,1},{25,9},{2,18},{10... | collective-permute-start | bytes 1216520 | tf_op jit(solution)/shard_map/ppermute | solution.py:311
  223.5 49.5 %collective-permute-start.27 = (bf16[528,384]{1,0:T(8,128)(2,1)}, bf16[528,384]{1,0:T(8,128)(2,1)}, u32[]{:S(2)}, u32[]{:S(2)}) collective-permute-start(bf16[528,384]{1,0:T(8,128)(2,1)} %shard_map.82), channel_id=1, source_target_pairs={{0,16},{8,24},{16,0},{24,8},{1,17},{9,25},{17,1},{25,9},{2,18},{10... | collective-permute-start | bytes 1216520 | tf_op jit(solution)/shard_map/ppermute | solution.py:311
  243.3 6.3 %copy-start = (bf16[1056,384]{1,0:T(8,128)(2,1)}, bf16[1056,384]{1,0:T(8,128)(2,1)S(1)}, u32[]{:S(2)}) copy-start(bf16[1056,384]{1,0:T(8,128)(2,1)S(1)} %collective-permute-done.10.refs_0_) | copy-start | bytes 2433028
  249.6 36.9 %collective-permute-start.11 = (bf16[528,384]{1,0:T(8,128)(2,1)}, bf16[528,384]{1,0:T(8,128)(2,1)S(1)}, u32[]{:S(2)}, u32[]{:S(2)}) collective-permute-start(bf16[528,384]{1,0:T(8,128)(2,1)} %shard_map.74), channel_id=1, source_target_pairs={{0,16},{8,24},{16,0},{24,8},{1,17},{9,25},{17,1},{25,9},{2,18},{10... | collective-permute-start | bytes 1216520 | tf_op jit(solution)/shard_map/ppermute | solution.py:311
  266.4 28.8 %collective-permute-start.25 = (bf16[528,384]{1,0:T(8,128)(2,1)}, bf16[528,384]{1,0:T(8,128)(2,1)}, u32[]{:S(2)}, u32[]{:S(2)}) collective-permute-start(bf16[528,384]{1,0:T(8,128)(2,1)} %shard_map.80), channel_id=1, source_target_pairs={{0,16},{8,24},{16,0},{24,8},{1,17},{9,25},{17,1},{25,9},{2,18},{10... | collective-permute-start | bytes 1216520 | tf_op jit(solution)/shard_map/ppermute | solution.py:311
  273.0 13.5 %copy-start.1 = (bf16[1056,384]{1,0:T(8,128)(2,1)S(1)}, bf16[1056,384]{1,0:T(8,128)(2,1)}, u32[]{:S(2)}) copy-start(bf16[1056,384]{1,0:T(8,128)(2,1)} %copy-done) | copy-start | bytes 2433028
  292.8 8.9 %copy-start.3 = (f32[1,16,384]{2,1,0:T(8,128)S(1)}, f32[1,16,384]{2,1,0:T(8,128)}, u32[]{:S(2)}) copy-start(f32[1,16,384]{2,1,0:T(8,128)} %shard_map.78) | copy-start | bytes 73732
  302.4 8.1 %copy-start.2 = (f32[2,16,384]{2,1,0:T(8,128)}, f32[2,16,384]{2,1,0:T(8,128)S(1)}, u32[]{:S(2)}) copy-start(f32[2,16,384]{2,1,0:T(8,128)S(1)} %pad_maximum_fusion.refs_0_) | copy-start | bytes 147460
  302.4 4.7 %collective-permute-start.28 = (f32[2,16,384]{2,1,0:T(8,128)S(1)}, f32[2,16,384]{2,1,0:T(8,128)S(1)}, u32[]{:S(2)}, u32[]{:S(2)}) collective-permute-start(f32[2,16,384]{2,1,0:T(8,128)S(1)} %pad_maximum_fusion.refs_0_), channel_id=1, source_target_pairs={{0,8},{8,0},{16,24},{24,16},{1,9},{9,1},{17,25},{25,17},{2,10},{10... | collective-permute-start | bytes 147464 | tf_op jit(solution)/shard_map/ppermute | solution.py:417
  302.5 5.7 %collective-permute-start.29 = (f32[2,16,384]{2,1,0:T(8,128)S(1)}, f32[2,16,384]{2,1,0:T(8,128)S(1)}, u32[]{:S(2)}, u32[]{:S(2)}) collective-permute-start(f32[2,16,384]{2,1,0:T(8,128)S(1)} %pad_maximum_fusion.refs_0_), channel_id=1, source_target_pairs={{0,16},{8,24},{16,0},{24,8},{1,17},{9,25},{17,1},{25,9},{2,18},{10... | collective-permute-start | bytes 147464 | tf_op jit(solution)/shard_map/ppermute | solution.py:417
  304.6 5.9 %collective-permute-start.30 = (f32[2,16,384]{2,1,0:T(8,128)S(1)}, f32[2,16,384]{2,1,0:T(8,128)S(1)}, u32[]{:S(2)}, u32[]{:S(2)}) collective-permute-start(f32[2,16,384]{2,1,0:T(8,128)S(1)} %pad_maximum_fusion.refs_0_), channel_id=1, source_target_pairs={{0,24},{8,16},{16,8},{24,0},{1,25},{9,17},{17,9},{25,1},{2,26},{10... | collective-permute-start | bytes 147464 | tf_op jit(solution)/shard_map/ppermute | solution.py:417
  307.1 3.4 %copy-start.4 = (f32[2,16,384]{2,1,0:T(8,128)}, f32[2,16,384]{2,1,0:T(8,128)S(1)}, u32[]{:S(2)}) copy-start(f32[2,16,384]{2,1,0:T(8,128)S(1)} %collective-permute-done.28.refs_1_) | copy-start | bytes 147460
  308.1 2.4 copy-start.5
  310.5 0.6 copy-start.6
